TPU v7x, 256 devices: a whole 4x4x8 slice. The times are simulated.
256 devices in a mesh: upd: 8 (over x, core), col: 32 (over z, y).
Axes of the slice: x: 4, y: 4, z: 8, core: 2. Of those that a mesh axis runs over, the one named last changes fastest.
Arguments:
- panel: bfloat16 [32, 8, 1024, 1024], P('col', None, 'upd'), may hold values from -6 to 6
- diag_tiles: bfloat16 [32, 1024, 1024], P('col', 'upd'), may hold values from -6 to 6
- dinv: bfloat16 [32, 1024, 1024], P('col'), may hold values from -1 to 1, as said below
- u_fac: bfloat16 [32, 8, 8, 96, 1024], P('col', None, 'upd'), may hold values from -1.1953125 to 1.1953125
- v_fac: bfloat16 [32, 8, 8, 96, 1024], P('col', None, 'upd'), may hold values from -1.1953125 to 1.1953125
- ranks: int32 [32, 8, 8], P('col', None, 'upd'), may hold values from 1 to 96, as said below
- sketch: bfloat16 [32, 64, 1024], P('col'), may hold values from -6 to 6
Outputs:
- panel_out: bfloat16 [32, 8, 1024, 1024], P('col', None, 'upd')
- diag_out: float32 [32, 1024, 1024], P('col', 'upd')
Inputs may be any that keep to these rules, and one draw needn't show every extreme that they name: `ranks`: in every panel tile at least two of the 8 pieces have rank 96. `dinv`: each block is lower triangular with a positive diagonal.
All inputs are finite; a program needn't handle non-finite values.
Results may differ from a plain program's by a relative error of at most 0.014.
Values may be sent and summed in bfloat16 or wider, within the bound.
No kernel may reach another device: no remote copies, remote signals or barrier semaphores. Data moves between devices by JAX's collectives and lax.ppermute only.
A program may use at most 64 MiB of HBM per device.

v0:
```python
import jax
import jax.numpy as jnp
from jax import lax
from jax.experimental import pallas as pl
from jax.experimental.pallas import tpu as pltpu
from jax.sharding import PartitionSpec as P


F32 = jnp.float32
BF16 = jnp.bfloat16
AXES = ("upd", "col")
NU = 8
NX = 4
NY = 4
NC = 32
HALF = 5
BLK = 128
NEAR = ((1,), (1,))
LEFT = ((0,), (0,))
EXACT = lax.Precision.HIGHEST


def dot(a, b, dims, precision=None):
    return lax.dot_general(a, b, (dims, ((), ())), precision=precision, preferred_element_type=F32)


def place():
    at = lax.axis_index("upd")
    return at >> 1, at & 1


def perm(block, route):
    pairs = []
    for u in range(NU):
        for c in range(NC):
            to = route(u, c)
            if to is not None:
                pairs.append((u * NC + c, to[0] * NC + to[1]))
    return lax.ppermute(block, AXES, pairs)


def along_x(k):
    return lambda u, c: ((u + 2 * k) % NU, c)


def along_upd(k):
    return lambda u, c: ((u + k) % NU, c)


def partner(u, c):
    return (u ^ 1, c)


def to_column(k):
    return lambda u, c: ((u + 2 * k) % NU, c // NY * NY + (c + u // 2 + 1) % NY)


def along_z(k):
    return lambda u, c: (u, (c + NY * k) % NC)


def call(kernel, outs, ins, scalars=(), scratch=(), in_hbm=False):
    vmem = pl.BlockSpec(memory_space=pltpu.VMEM)
    if in_hbm:
        shapes = [jax.ShapeDtypeStruct(*out) for out in outs]
    else:
        shapes = [pltpu.VMEM(*out) for out in outs]
    out_spec = pl.BlockSpec(memory_space=pl.ANY) if in_hbm else vmem
    return pl.pallas_call(
        kernel,
        out_shape=shapes,
        in_specs=[pl.BlockSpec(memory_space=pltpu.SMEM)] * len(scalars) + [vmem] * len(ins),
        out_specs=[out_spec] * len(outs),
        scratch_shapes=list(scratch),
        compiler_params=pltpu.CompilerParams(vmem_limit_bytes=16 * 1024 * 1024),
    )(*scalars, *[pltpu.with_memory_space_constraint(x, pltpu.VMEM) for x in ins])


def masked(probe, rank):
    slots = lax.broadcasted_iota(jnp.int32, probe.shape, 0)
    return jnp.where(slots < rank, probe, 0.0).astype(BF16)


def sketch_kernel(ranks, v_hbm, u_hbm, sketch_hbm, send_ref, keep_ref, v_ref, u_ref, sketch_ref, sems):
    x, core = place()
    order = [(k, other) for k in range(NX) for other in (1, 0)]
    tiles = [((x + k) & 3) + 4 * (core ^ other) for k, other in order]
    first = pltpu.make_async_copy(sketch_hbm, sketch_ref, sems.at[2 * NU])
    first.start()
    copies = []
    for i, tile in enumerate(tiles):
        pair = (
            pltpu.make_async_copy(v_hbm.at[tile], v_ref.at[i], sems.at[2 * i]),
            pltpu.make_async_copy(u_hbm.at[tile], u_ref.at[i], sems.at[2 * i + 1]),
        )
        for copy in pair:
            copy.start()
        copies.append(pair)
    first.wait()
    for i, (k, other) in enumerate(order):
        copies[i][0].wait()
        probe = masked(dot(v_ref[i], sketch_ref[...], NEAR), ranks[tiles[i]])
        copies[i][1].wait()
        out = dot(probe, u_ref[i], LEFT)
        if other:
            send_ref[k] = out.astype(BF16)
        else:
            keep_ref[k] = out


def sketch_call(ranks, v, u, sketch):
    vmem = pl.BlockSpec(memory_space=pltpu.VMEM)
    hbm = pl.BlockSpec(memory_space=pltpu.HBM)
    out = (NX,) + sketch.shape
    return pl.pallas_call(
        sketch_kernel,
        out_shape=[pltpu.VMEM(out, BF16), pltpu.VMEM(out, F32)],
        in_specs=[pl.BlockSpec(memory_space=pltpu.SMEM)] + [hbm] * 3,
        out_specs=[vmem] * 2,
        scratch_shapes=[
            pltpu.VMEM(v.shape, BF16),
            pltpu.VMEM(u.shape, BF16),
            pltpu.VMEM(sketch.shape, BF16),
            pltpu.SemaphoreType.DMA((2 * NU + 1,)),
        ],
        compiler_params=pltpu.CompilerParams(vmem_limit_bytes=16 * 1024 * 1024),
        name="sketch_product",
    )(ranks, *[pltpu.with_memory_space_constraint(x, pltpu.HBM) for x in (v, u, sketch)])


def project_kernel(ranks, u_ref, v_ref, *refs):
    bases, (send_ref, keep_ref) = refs[:NU], refs[NU:]
    x, core = place()
    for d in range(NX):
        for other in range(2):
            tile = ((x - d) & 3) + 4 * (core ^ other)
            basis = bases[NX * other + d][...]
            coeff = masked(dot(u_ref[tile], basis, NEAR), ranks[tile])
            out = dot(coeff, v_ref[tile], LEFT)
            if other:
                send_ref[-d % NX] = out.astype(BF16)
            else:
                keep_ref[-d % NX] = out


def sum_product(split, ranks, u, v, sums):
    return call(project_kernel, split, [u, v, *sums], [ranks])


def pair_sum_kernel(keep_ref, got_ref, own_ref, a_ref, b_ref, c_ref):
    for k, ref in enumerate((own_ref, a_ref, b_ref, c_ref)):
        ref[...] = (keep_ref[k] + got_ref[k].astype(F32)).astype(ref.dtype)


def pair_sum(keep, got):
    shape = keep.shape[1:]
    outs = [(shape, F32)] + [(shape, BF16)] * (NX - 1)
    return call(pair_sum_kernel, outs, [keep, got])


def owner_sum(own_ref, *others):
    total = own_ref[...]
    for ref in others:
        total = total + ref[...].astype(F32)
    return total


def summed_kernel(own_ref, a_ref, b_ref, c_ref, summed_ref):
    summed_ref[...] = owner_sum(own_ref, a_ref, b_ref, c_ref).astype(BF16)


def owner_total(own, others):
    return call(summed_kernel, [(own.shape, BF16)], [own, *others])[0]


def inverse_kernel(summed_ref, inverse_ref):
    summed = summed_ref[...].astype(F32)
    rk = summed.shape[0]
    gram = dot(summed, summed, NEAR, EXACT)
    rows = lax.broadcasted_iota(jnp.int32, (rk, rk), 0)
    cols = lax.broadcasted_iota(jnp.int32, (rk, rk), 1)
    row_at = lax.broadcasted_iota(jnp.int32, (rk, 1), 0)
    work = jnp.concatenate([gram, jnp.where(rows == cols, 1.0, 0.0)], axis=1)
    for k in range(rk):
        row = work[k : k + 1, :]
        scaled = row * (1.0 / work[k : k + 1, k : k + 1])
        col = jnp.where(row_at > k, work[:, k : k + 1], 0.0)
        work = work - col * scaled
    pivots = jnp.sum(jnp.where(rows == cols, work[:, :rk], 0.0), axis=1, keepdims=True)
    half = work[:, rk:] * lax.rsqrt(pivots)
    inverse_ref[...] = dot(half, half, LEFT, EXACT)


def cross_kernel(inverse_ref, own_ref, a_ref, b_ref, c_ref, cross_ref):
    raw = owner_sum(own_ref, a_ref, b_ref, c_ref)
    cross_ref[...] = dot(inverse_ref[...], raw, ((1,), (0,)), EXACT).astype(BF16)


def gram_inverse(summed):
    rk = summed.shape[0]
    return call(inverse_kernel, [((rk, rk), F32)], [summed])[0]


def cross_total(inverse, own, others):
    return call(cross_kernel, [(own.shape, BF16)], [inverse, own, *others])[0]


def split_kernel(panel_ref, send_ref, keep_ref):
    x, core = place()
    for k in range(NX):
        tile = (x + k) & 3
        send_ref[k] = panel_ref[tile + 4 * (core ^ 1)]
        keep_ref[k] = panel_ref[tile + 4 * core]


def bundle_kernel(keep_ref, got_ref, *outs):
    for k, ref in enumerate(outs):
        ref[0] = keep_ref[NX - len(outs) + k]
        ref[1] = got_ref[NX - len(outs) + k]


def bundles(keep, got, first):
    shape = ((2,) + keep.shape[1:], BF16)
    return call(bundle_kernel, [shape] * (NX - first), [keep, got])


def split_panel(panel):
    shape = ((NX,) + panel.shape[1:], BF16)
    return call(split_kernel, [shape] * 2, [panel])


def tile_kernel(basis_ref, cross_ref, dinv_ref, keep_ref, got_ref, a_ref, b_ref, c_ref, send_out, keep_out, updated, solved):
    x, core = place()
    lowrank = dot(basis_ref[...], cross_ref[...], LEFT)
    updated[...] = lowrank
    for d in range(NX):
        for other in range(2):
            at = pl.multiple_of((2 * ((x - d) & 3) + (core ^ other)) * BLK, BLK)
            if d:
                rows = (a_ref, b_ref, c_ref)[d - 1][other]
            else:
                rows = (keep_ref, got_ref)[other][0]
            updated[pl.ds(at, BLK)] = rows.astype(F32) - updated[pl.ds(at, BLK)]
    wrap = (HALF - 1) * BLK
    result = dot(updated[...].astype(BF16), dinv_ref[...], NEAR).astype(BF16)
    solved[wrap:] = result
    solved[:wrap] = result[-wrap:]
    for k in range(NX):
        at = pl.multiple_of(((x + k) & 3) * (2 * BLK), 2 * BLK)
        product = dot(solved[pl.ds(at + wrap, 2 * BLK)], solved[pl.ds(at, (HALF + 1) * BLK)], NEAR)
        upper = product[:BLK, : HALF * BLK].astype(BF16)
        lower = product[BLK:, BLK:].astype(BF16)
        on_lower = core == 1
        keep_out[k] = jnp.where(on_lower, lower, upper)
        send_out[k] = jnp.where(on_lower, upper, lower)


def tile_call(basis, cross, dinv, rows):
    width = dinv.shape[0]
    out = ((NX, BLK, HALF * BLK), BF16)
    return call(
        tile_kernel,
        [out, out],
        [basis, cross, dinv, *rows],
        scratch=[
            pltpu.VMEM((width, width), F32),
            pltpu.VMEM((width + (HALF - 1) * BLK, width), BF16),
        ],
    )


def rows_kernel(panel_ref, dinv_ref, *refs):
    bases, crosses = refs[:NU], refs[NU : 2 * NU]
    out_ref, updated, solved, sems = refs[2 * NU :]
    x, core = place()
    at = pl.multiple_of((2 * x + core) * BLK, BLK)
    copies = []
    for d in range(NX):
        for other in range(2):
            tile = ((x - d) & 3) + 4 * (core ^ other)
            source = NX * other + d
            lowrank = dot(bases[source][:, pl.ds(at, BLK)], crosses[source][...], LEFT)
            rows = (panel_ref[tile].astype(F32) - lowrank).astype(BF16)
            updated[other * BLK : (other + 1) * BLK] = rows
        result = dot(updated[...], dinv_ref[...], NEAR).astype(BF16)
        for other in range(2):
            tile = ((x - d) & 3) + 4 * (core ^ other)
            slot = 2 * d + other
            solved[slot] = result[other * BLK : (other + 1) * BLK]
            copy = pltpu.make_async_copy(solved.at[slot], out_ref.at[tile], sems.at[slot])
            copy.start()
            copies.append(copy)
    for copy in copies:
        copy.wait()


def rows_call(panel, dinv, bases, crosses):
    return call(
        rows_kernel,
        [(panel.shape, BF16)],
        [panel, dinv, *bases, *crosses],
        scratch=[
            pltpu.VMEM((2 * BLK, panel.shape[2]), BF16),
            pltpu.VMEM(panel.shape, BF16),
            pltpu.SemaphoreType.DMA((NU,)),
        ],
        in_hbm=True,
    )[0]


def arrived_kernel(a_ref, b_ref, c_ref, d_ref, here_ref, one_ref, two_ref):
    x, core = place()
    y = lax.axis_index("col") & 3
    here = one = two = None
    for k, ref in enumerate((a_ref, b_ref, c_ref, d_ref)):
        stays = y > ((x - k) & 3)
        near, far = ref[core].astype(F32), ref[core ^ 1].astype(F32)
        parts = (jnp.where(stays, near, 0.0), jnp.where(stays, far, near), jnp.where(stays, 0.0, far))
        here, one, two = parts if k == 0 else (here + parts[0], one + parts[1], two + parts[2])
    here_ref[...] = here
    one_ref[...] = one.astype(BF16)
    two_ref[...] = two.astype(BF16)


def arrived_sum(arrived):
    shape = arrived[0].shape[1:]
    outs = [(shape, F32), (shape, BF16), (shape, BF16)]
    return call(arrived_kernel, outs, arrived)


def collect_kernel(here_ref, one_ref, two_ref, total_ref, a_ref, b_ref, c_ref):
    z = lax.axis_index("col") >> 2
    total = here_ref[...] + jnp.where(z >= 1, one_ref[...].astype(F32), 0.0)
    total = total + jnp.where(z >= 2, two_ref[...].astype(F32), 0.0)
    total_ref[...] = total
    for d, ref in ((1, a_ref), (2, b_ref), (3, c_ref)):
        i = HALF - 1 - d
        ref[...] = total[:, i * BLK : (i + 1) * BLK].T


def collect(here, onward):
    outs = [(here.shape, F32)] + [((BLK, BLK), F32)] * (HALF - 2)
    return call(collect_kernel, outs, [here, *onward])


def diag_kernel(diag_ref, total_ref, a_ref, b_ref, c_ref, out_ref):
    x, core = place()
    u = 2 * x + core
    for i in range(HALF):
        at = pl.ds(pl.multiple_of(((u + i + 4) & 7) * BLK, BLK), BLK)
        out_ref[:, at] = diag_ref[:, at].astype(F32) - total_ref[:, i * BLK : (i + 1) * BLK]
    for d, ref in ((1, a_ref), (2, b_ref), (3, c_ref)):
        at = pl.ds(pl.multiple_of(((u + d) & 7) * BLK, BLK), BLK)
        out_ref[:, at] = diag_ref[:, at].astype(F32) - ref[...]


def diag_call(diag, total, mirrored):
    vmem = pl.BlockSpec(memory_space=pltpu.VMEM)
    ins = [diag, total, *mirrored]
    return pl.pallas_call(
        diag_kernel,
        out_shape=jax.ShapeDtypeStruct(diag.shape, F32),
        in_specs=[vmem] * len(ins),
        out_specs=vmem,
        compiler_params=pltpu.CompilerParams(vmem_limit_bytes=16 * 1024 * 1024),
        name="diagonal",
    )(*[pltpu.with_memory_space_constraint(x, pltpu.VMEM) for x in ins])


def shifted(blocks, route, first=1):
    return [perm(block, route(i)) for i, block in enumerate(blocks, start=first)]


def gathered(own):
    mine = [own] + shifted([own] * (NX - 1), along_x)
    return mine + shifted(mine, lambda i: partner, 0)


def local(panel, diag_tiles, dinv, u_fac, v_fac, ranks, sketch):
    panel, dinv = panel[0], dinv[0]
    u, v, ranks = u_fac[0, :, 0], v_fac[0, :, 0], ranks[0, :, 0]
    small = sketch.shape[1:]
    split = [((NX,) + small, BF16), ((NX,) + small, F32)]

    send, keep = sketch_call(ranks, v, u, sketch[0])
    got = perm(send, partner)
    panel_send, panel_keep = split_panel(panel)
    panel_got = perm(panel_send, partner)
    own, *others = pair_sum(keep, got)
    others = shifted(others, along_x)
    panel_bundles = bundles(panel_keep, panel_got, 1)
    rows = [panel_keep, panel_got] + shifted(panel_bundles, along_x)
    own_sum = owner_total(own, others)
    sums = gathered(own_sum)
    inverse = gram_inverse(own_sum)
    send, keep = sum_product(split, ranks, u, v, sums)
    got = perm(send, partner)
    own, *others = pair_sum(keep, got)
    others = shifted(others, along_x)
    cross = cross_total(inverse, own, others)
    send, keep = tile_call(own_sum, cross, dinv, rows)
    got = perm(send, partner)
    blocks = bundles(keep, got, 0)
    arrived = shifted(blocks, to_column, 0)
    crosses = gathered(cross)
    here, *onward = arrived_sum(arrived)
    onward = shifted(onward, along_z)
    total, *mirrored = collect(here, onward)
    mirrored = shifted(mirrored, lambda d: along_upd(-d))
    panel_out = rows_call(panel, dinv, sums, crosses)
    diag_out = diag_call(diag_tiles[0], total, mirrored)
    return (panel_out[None], diag_out[None])


def solution(mesh):
    in_specs = (
        P("col", None, "upd", None),
        P("col", "upd", None),
        P("col", None, None),
        P("col", None, "upd", None, None),
        P("col", None, "upd", None, None),
        P("col", None, "upd"),
        P("col", None, None),
    )
    out_specs = (P("col", None, "upd", None), P("col", "upd", None))
    return jax.shard_map(local, mesh=mesh, in_specs=in_specs, out_specs=out_specs, check_vma=False)
```

profile of v0, /device:TPU:41, one launch (start us, length us, event | category | flops | bytes accessed | tf_op | source)
XLA Modules:
  0.0 136.7 jit_solution(14749697525394586799)
XLA Ops:
  1.4 5.4 %sketch_product.1 = (bf16[4,64,1024]{2,1,0:T(8,128)(2,1)S(1)}, f32[4,64,1024]{2,1,0:T(8,128)S(1)}) custom-call(s32[8]{0:T(128)S(1)} %bitcast.18, bf16[8,96,1024]{2,1,0:T(8,128)(2,1)} %bitcast.13, bf16[8,96,1024]{2,1,0:T(8,128)(2,1)} %bitcast.15, bf16[64,1024]{1,0:T(8,128)(2,1)} %bitcast.22), custom_call_target="tpu_custom_call" | custom-call | tf_op jit(solution)/shard_map/sketch_product/pallas_call | solution.py:115
  8.0 1.2 collective-permute-done.got_ref
  9.3 1.3 collective-permute-start.1
  10.6 2.4 %collective-permute-start.2 = (bf16[64,1024]{1,0:T(8,128)(2,1)S(1)}, bf16[64,1024]{1,0:T(8,128)(2,1)S(1)}, u32[]{:S(2)}, u32[]{:S(2)}) collective-permute-start(bf16[64,1024]{1,0:T(8,128)(2,1)S(1)} %get-tuple-element.36), channel_id=1, source_target_pairs={{0,128},{1,129},{2,130},{3,131},{4,132},{5,133},{6,134},{7,135},{8... | collective-permute-start | bytes 393224 | tf_op jit(solution)/shard_map/ppermute | solution.py:39
  15.3 3.8 %collective-permute-done.2.b_ref = bf16[64,1024]{1,0:T(8,128)(2,1)S(1)} collective-permute-done((bf16[64,1024]{1,0:T(8,128)(2,1)S(1)}, bf16[64,1024]{1,0:T(8,128)(2,1)S(1)}, u32[]{:S(2)}, u32[]{:S(2)}) %collective-permute-start.2) | collective-permute-done | bytes 131104 | tf_op jit(solution)/shard_map/ppermute | solution.py:39
  19.1 2.2 %collective-permute-start.6 = (bf16[64,1024]{1,0:T(8,128)(2,1)S(1)}, bf16[64,1024]{1,0:T(8,128)(2,1)S(1)}, u32[]{:S(2)}, u32[]{:S(2)}) collective-permute-start(bf16[64,1024]{1,0:T(8,128)(2,1)S(1)} %shard_map.87.summed_ref.refs_0_.basis_ref), channel_id=1, source_target_pairs={{0,192},{1,193},{2,194},{3,195},{4,196},{5,197},{6,198},{7,199},{8... | collective-permute-start | bytes 393224 | tf_op jit(solution)/shard_map/ppermute | solution.py:39
  21.3 1.5 %collective-permute-start.5 = (bf16[64,1024]{1,0:T(8,128)(2,1)S(1)}, bf16[64,1024]{1,0:T(8,128)(2,1)S(1)}, u32[]{:S(2)}, u32[]{:S(2)}) collective-permute-start(bf16[64,1024]{1,0:T(8,128)(2,1)S(1)} %shard_map.87.summed_ref.refs_0_.basis_ref), channel_id=1, source_target_pairs={{0,128},{1,129},{2,130},{3,131},{4,132},{5,133},{6,134},{7,135},{8... | collective-permute-start | bytes 393224 | tf_op jit(solution)/shard_map/ppermute | solution.py:39
  22.8 2.3 %collective-permute-start.7 = (bf16[64,1024]{1,0:T(8,128)(2,1)S(1)}, bf16[64,1024]{1,0:T(8,128)(2,1)S(1)}, u32[]{:S(2)}, u32[]{:S(2)}) collective-permute-start(bf16[64,1024]{1,0:T(8,128)(2,1)S(1)} %shard_map.87.summed_ref.refs_0_.basis_ref), channel_id=1, source_target_pairs={{0,32},{1,33},{2,34},{3,35},{4,36},{5,37},{6,38},{7,39},{8,40},{9,... | collective-permute-start | bytes 393224 | tf_op jit(solution)/shard_map/ppermute | solution.py:39
  25.4 4.8 %collective-permute-done.4.refs_1_ = bf16[64,1024]{1,0:T(8,128)(2,1)S(1)} collective-permute-done((bf16[64,1024]{1,0:T(8,128)(2,1)S(1)}, bf16[64,1024]{1,0:T(8,128)(2,1)S(1)}, u32[]{:S(2)}, u32[]{:S(2)}) %collective-permute-start.4) | collective-permute-done | bytes 131104 | tf_op jit(solution)/shard_map/ppermute | solution.py:39
  32.6 3.1 %shard_map.89 = (bf16[4,64,1024]{2,1,0:T(8,128)(2,1)S(1)}, f32[4,64,1024]{2,1,0:T(8,128)S(1)}) custom-call(s32[8]{0:T(128)S(1)} %bitcast.19, bf16[8,96,1024]{2,1,0:T(8,128)(2,1)S(1)} %bitcast.16, bf16[8,96,1024]{2,1,0:T(8,128)(2,1)S(1)} %bitcast.14, bf16[64,1024]{1,0:T(8,128)(2,1)S(1)} %shard_map.87.summed_ref.refs_0_.basis_ref, ...), custom_call_target="tpu_custom_call" | custom-call | tf_op jit(solution)/shard_map/pallas_call | solution.py:69
  36.2 1.8 %collective-permute-start.24 = (bf16[2,128,1024]{2,1,0:T(8,128)(2,1)S(1)}, bf16[2,128,1024]{2,1,0:T(8,128)(2,1)S(1)}, u32[]{:S(2)}, u32[]{:S(2)}) collective-permute-start(bf16[2,128,1024]{2,1,0:T(8,128)(2,1)S(1)} %get-tuple-element.47), channel_id=1, source_target_pairs={{0,128},{1,129},{2,130},{3,131},{4,132},{5,133},{6,134},{7,135},{8... | collective-permute-start | bytes 1572872 | tf_op jit(solution)/shard_map/ppermute | solution.py:39
  39.7 1.8 %collective-permute-start.13 = (bf16[64,1024]{1,0:T(8,128)(2,1)S(1)}, bf16[64,1024]{1,0:T(8,128)(2,1)S(1)}, u32[]{:S(2)}, u32[]{:S(2)}) collective-permute-start(bf16[64,1024]{1,0:T(8,128)(2,1)S(1)} %get-tuple-element.42), channel_id=1, source_target_pairs={{0,128},{1,129},{2,130},{3,131},{4,132},{5,133},{6,134},{7,135},{8... | collective-permute-start | bytes 393224 | tf_op jit(solution)/shard_map/ppermute | solution.py:39
  41.5 23.7 %collective-permute-done.12.a_ref = bf16[64,1024]{1,0:T(8,128)(2,1)S(1)} collective-permute-done((bf16[64,1024]{1,0:T(8,128)(2,1)S(1)}, bf16[64,1024]{1,0:T(8,128)(2,1)S(1)}, u32[]{:S(2)}, u32[]{:S(2)}) %collective-permute-start.12) | collective-permute-done | bytes 131104 | tf_op jit(solution)/shard_map/ppermute | solution.py:39
  65.2 6.1 %shard_map.88.inverse_ref = f32[64,64]{1,0:T(8,128)S(1)} custom-call(bf16[64,1024]{1,0:T(8,128)(2,1)S(1)} %shard_map.87.summed_ref.refs_0_.basis_ref), custom_call_target="tpu_custom_call" | custom-call | tf_op jit(solution)/shard_map/pallas_call | solution.py:69
  71.7 5.2 %shard_map.95 = (bf16[4,128,640]{2,1,0:T(8,128)(2,1)S(1)}, bf16[4,128,640]{2,1,0:T(8,128)(2,1)S(1)}) custom-call(bf16[64,1024]{1,0:T(8,128)(2,1)S(1)} %shard_map.87.summed_ref.refs_0_.basis_ref, bf16[64,1024]{1,0:T(8,128)(2,1)S(1)} %shard_map.91.refs_8_.cross_ref, bf16[1024,1024]{1,0:T(8,128)(2,1)S(1)} %bitcast.9, ...), custom_call_target="tpu_custom_call" | custom-call | tf_op jit(solution)/shard_map/pallas_call | solution.py:69
  76.8 3.5 %collective-permute-start.26 = (bf16[4,128,640]{2,1,0:T(8,128)(2,1)S(1)}, bf16[4,128,640]{2,1,0:T(8,128)(2,1)S(1)}, u32[]{:S(2)}, u32[]{:S(2)}) collective-permute-start(bf16[4,128,640]{2,1,0:T(8,128)(2,1)S(1)} %get-tuple-element.50), channel_id=1, source_target_pairs={{0,32},{1,33},{2,34},{3,35},{4,36},{5,37},{6,38},{7,39},{8,40},{9,... | collective-permute-start | bytes 1966088 | tf_op jit(solution)/shard_map/ppermute | solution.py:39
  80.3 1.7 %collective-permute-done.26.got_ref = bf16[4,128,640]{2,1,0:T(8,128)(2,1)S(1)} collective-permute-done((bf16[4,128,640]{2,1,0:T(8,128)(2,1)S(1)}, bf16[4,128,640]{2,1,0:T(8,128)(2,1)S(1)}, u32[]{:S(2)}, u32[]{:S(2)}) %collective-permute-start.26) | collective-permute-done | bytes 655392 | tf_op jit(solution)/shard_map/ppermute | solution.py:39
  82.2 3.2 %collective-permute-start.27 = (bf16[2,128,640]{2,1,0:T(8,128)(2,1)S(1)}, bf16[2,128,640]{2,1,0:T(8,128)(2,1)S(1)}, u32[]{:S(2)}, u32[]{:S(2)}) collective-permute-start(bf16[2,128,640]{2,1,0:T(8,128)(2,1)S(1)} %get-tuple-element.51), channel_id=1, source_target_pairs={{0,1},{1,2},{2,3},{3,0},{4,5},{5,6},{6,7},{7,4},{8,9},{9,10},{10,1... | collective-permute-start | bytes 983048 | tf_op jit(solution)/shard_map/ppermute | solution.py:39
  85.4 1.6 %collective-permute-start.28 = (bf16[2,128,640]{2,1,0:T(8,128)(2,1)S(1)}, bf16[2,128,640]{2,1,0:T(8,128)(2,1)S(1)}, u32[]{:S(2)}, u32[]{:S(2)}) collective-permute-start(bf16[2,128,640]{2,1,0:T(8,128)(2,1)S(1)} %get-tuple-element.52), channel_id=1, source_target_pairs={{0,65},{1,66},{2,67},{3,64},{4,69},{5,70},{6,71},{7,68},{8,73},{9,... | collective-permute-start | bytes 983048 | tf_op jit(solution)/shard_map/ppermute | solution.py:39
  87.0 2.5 %collective-permute-start.30 = (bf16[2,128,640]{2,1,0:T(8,128)(2,1)S(1)}, bf16[2,128,640]{2,1,0:T(8,128)(2,1)S(1)}, u32[]{:S(2)}, u32[]{:S(2)}) collective-permute-start(bf16[2,128,640]{2,1,0:T(8,128)(2,1)S(1)} %get-tuple-element.54), channel_id=1, source_target_pairs={{0,193},{1,194},{2,195},{3,192},{4,197},{5,198},{6,199},{7,196},{8... | collective-permute-start | bytes 983048 | tf_op jit(solution)/shard_map/ppermute | solution.py:39
  89.4 2.2 %collective-permute-start.15 = (bf16[64,1024]{1,0:T(8,128)(2,1)S(1)}, bf16[64,1024]{1,0:T(8,128)(2,1)S(1)}, u32[]{:S(2)}, u32[]{:S(2)}) collective-permute-start(bf16[64,1024]{1,0:T(8,128)(2,1)S(1)} %shard_map.91.refs_8_.cross_ref), channel_id=1, source_target_pairs={{0,64},{1,65},{2,66},{3,67},{4,68},{5,69},{6,70},{7,71},{8,72},{9,... | collective-permute-start | bytes 393224 | tf_op jit(solution)/shard_map/ppermute | solution.py:39
  91.7 1.3 collective-permute-done.27.a_ref
  93.3 9.8 %collective-permute-done.28.b_ref = bf16[2,128,640]{2,1,0:T(8,128)(2,1)S(1)} collective-permute-done((bf16[2,128,640]{2,1,0:T(8,128)(2,1)S(1)}, bf16[2,128,640]{2,1,0:T(8,128)(2,1)S(1)}, u32[]{:S(2)}, u32[]{:S(2)}) %collective-permute-start.28) | collective-permute-done | bytes 327712 | tf_op jit(solution)/shard_map/ppermute | solution.py:39
  103.0 3.8 %collective-permute-done.30.d_ref = bf16[2,128,640]{2,1,0:T(8,128)(2,1)S(1)} collective-permute-done((bf16[2,128,640]{2,1,0:T(8,128)(2,1)S(1)}, bf16[2,128,640]{2,1,0:T(8,128)(2,1)S(1)}, u32[]{:S(2)}, u32[]{:S(2)}) %collective-permute-start.30) | collective-permute-done | bytes 327712 | tf_op jit(solution)/shard_map/ppermute | solution.py:39
  107.2 1.7 %collective-permute-start.31 = (bf16[128,640]{1,0:T(8,128)(2,1)S(1)}, bf16[128,640]{1,0:T(8,128)(2,1)S(1)}, u32[]{:S(2)}, u32[]{:S(2)}) collective-permute-start(bf16[128,640]{1,0:T(8,128)(2,1)S(1)} %get-tuple-element.56), channel_id=1, source_target_pairs={{0,4},{1,5},{2,6},{3,7},{4,8},{5,9},{6,10},{7,11},{8,12},{9,13},{1... | collective-permute-start | bytes 491528 | tf_op jit(solution)/shard_map/ppermute | solution.py:39
  108.9 5.8 %collective-permute-start.17 = (bf16[64,1024]{1,0:T(8,128)(2,1)S(1)}, bf16[64,1024]{1,0:T(8,128)(2,1)S(1)}, u32[]{:S(2)}, u32[]{:S(2)}) collective-permute-start(bf16[64,1024]{1,0:T(8,128)(2,1)S(1)} %shard_map.91.refs_8_.cross_ref), channel_id=1, source_target_pairs={{0,192},{1,193},{2,194},{3,195},{4,196},{5,197},{6,198},{7,199},{8... | collective-permute-start | bytes 393224 | tf_op jit(solution)/shard_map/ppermute | solution.py:39
  114.8 4.2 %collective-permute-start.32 = (bf16[128,640]{1,0:T(8,128)(2,1)S(1)}, bf16[128,640]{1,0:T(8,128)(2,1)S(1)}, u32[]{:S(2)}, u32[]{:S(2)}) collective-permute-start(bf16[128,640]{1,0:T(8,128)(2,1)S(1)} %get-tuple-element.57), channel_id=1, source_target_pairs={{0,8},{1,9},{2,10},{3,11},{4,12},{5,13},{6,14},{7,15},{8,16},{9,17... | collective-permute-start | bytes 491528 | tf_op jit(solution)/shard_map/ppermute | solution.py:39
  119.0 1.3 collective-permute-start.18
  120.9 4.3 %collective-permute-done.32.two_ref = bf16[128,640]{1,0:T(8,128)(2,1)S(1)} collective-permute-done((bf16[128,640]{1,0:T(8,128)(2,1)S(1)}, bf16[128,640]{1,0:T(8,128)(2,1)S(1)}, u32[]{:S(2)}, u32[]{:S(2)}) %collective-permute-start.32) | collective-permute-done | bytes 163872 | tf_op jit(solution)/shard_map/ppermute | solution.py:39
  125.4 1.8 %collective-permute-start.33 = (f32[128,128]{1,0:T(8,128)S(1)}, f32[128,128]{1,0:T(8,128)S(1)}, u32[]{:S(2)}, u32[]{:S(2)}) collective-permute-start(f32[128,128]{1,0:T(8,128)S(1)} %get-tuple-element.59), channel_id=1, source_target_pairs={{0,224},{1,225},{2,226},{3,227},{4,228},{5,229},{6,230},{7,231},{8... | collective-permute-start | bytes 196616 | tf_op jit(solution)/shard_map/ppermute | solution.py:39
  127.2 3.4 %collective-permute-start.34 = (f32[128,128]{1,0:T(8,128)S(1)}, f32[128,128]{1,0:T(8,128)S(1)}, u32[]{:S(2)}, u32[]{:S(2)}) collective-permute-start(f32[128,128]{1,0:T(8,128)S(1)} %get-tuple-element.60), channel_id=1, source_target_pairs={{0,192},{1,193},{2,194},{3,195},{4,196},{5,197},{6,198},{7,199},{8... | collective-permute-start | bytes 196616 | tf_op jit(solution)/shard_map/ppermute | solution.py:39
  130.7 4.0 %shard_map.92 = bf16[8,128,1024]{2,1,0:T(8,128)(2,1)} custom-call(bf16[8,128,1024]{2,1,0:T(8,128)(2,1)S(1)} %bitcast.12, bf16[1024,1024]{1,0:T(8,128)(2,1)S(1)} %bitcast.10, bf16[64,1024]{1,0:T(8,128)(2,1)S(1)} %shard_map.87.summed_ref.refs_0_.basis_ref, bf16[64,1024]{1,0:T(8,128)(2,1)S(1)} %collective-permute-done.4.refs_1_, ...), custom_call_target="tpu_custom_call" | custom-call | tf_op jit(solution)/shard_map/pallas_call | solution.py:69
  (69 shorter events, 13.1 us)
Async XLA Ops:
  7.8 28.2 %collective-permute-start.22 = (bf16[4,128,1024]{2,1,0:T(8,128)(2,1)S(1)}, bf16[4,128,1024]{2,1,0:T(8,128)(2,1)S(1)}, u32[]{:S(2)}, u32[]{:S(2)}) collective-permute-start(bf16[4,128,1024]{2,1,0:T(8,128)(2,1)S(1)} %get-tuple-element.45), channel_id=1, source_target_pairs={{0,32},{1,33},{2,34},{3,35},{4,36},{5,37},{6,38},{7,39},{8,40},{9,... | collective-permute-start | bytes 3145736 | tf_op jit(solution)/shard_map/ppermute | solution.py:39
  9.3 6.0 %collective-permute-start.1 = (bf16[64,1024]{1,0:T(8,128)(2,1)S(1)}, bf16[64,1024]{1,0:T(8,128)(2,1)S(1)}, u32[]{:S(2)}, u32[]{:S(2)}) collective-permute-start(bf16[64,1024]{1,0:T(8,128)(2,1)S(1)} %get-tuple-element.35), channel_id=1, source_target_pairs={{0,64},{1,65},{2,66},{3,67},{4,68},{5,69},{6,70},{7,71},{8,72},{9,... | collective-permute-start | bytes 393224 | tf_op jit(solution)/shard_map/ppermute | solution.py:39
  10.6 8.5 %collective-permute-start.2 = (bf16[64,1024]{1,0:T(8,128)(2,1)S(1)}, bf16[64,1024]{1,0:T(8,128)(2,1)S(1)}, u32[]{:S(2)}, u32[]{:S(2)}) collective-permute-start(bf16[64,1024]{1,0:T(8,128)(2,1)S(1)} %get-tuple-element.36), channel_id=1, source_target_pairs={{0,128},{1,129},{2,130},{3,131},{4,132},{5,133},{6,134},{7,135},{8... | collective-permute-start | bytes 393224 | tf_op jit(solution)/shard_map/ppermute | solution.py:39
  13.0 6.0 %collective-permute-start.3 = (bf16[64,1024]{1,0:T(8,128)(2,1)S(1)}, bf16[64,1024]{1,0:T(8,128)(2,1)S(1)}, u32[]{:S(2)}, u32[]{:S(2)}) collective-permute-start(bf16[64,1024]{1,0:T(8,128)(2,1)S(1)} %get-tuple-element.37), channel_id=1, source_target_pairs={{0,192},{1,193},{2,194},{3,195},{4,196},{5,197},{6,198},{7,199},{8... | collective-permute-start | bytes 393224 | tf_op jit(solution)/shard_map/ppermute | solution.py:39
  19.1 6.0 %collective-permute-start.6 = (bf16[64,1024]{1,0:T(8,128)(2,1)S(1)}, bf16[64,1024]{1,0:T(8,128)(2,1)S(1)}, u32[]{:S(2)}, u32[]{:S(2)}) collective-permute-start(bf16[64,1024]{1,0:T(8,128)(2,1)S(1)} %shard_map.87.summed_ref.refs_0_.basis_ref), channel_id=1, source_target_pairs={{0,192},{1,193},{2,194},{3,195},{4,196},{5,197},{6,198},{7,199},{8... | collective-permute-start | bytes 393224 | tf_op jit(solution)/shard_map/ppermute | solution.py:39
  21.3 8.8 %collective-permute-start.4 = (bf16[64,1024]{1,0:T(8,128)(2,1)S(1)}, bf16[64,1024]{1,0:T(8,128)(2,1)S(1)}, u32[]{:S(2)}, u32[]{:S(2)}) collective-permute-start(bf16[64,1024]{1,0:T(8,128)(2,1)S(1)} %shard_map.87.summed_ref.refs_0_.basis_ref), channel_id=1, source_target_pairs={{0,64},{1,65},{2,66},{3,67},{4,68},{5,69},{6,70},{7,71},{8,72},{9,... | collective-permute-start | bytes 393224 | tf_op jit(solution)/shard_map/ppermute | solution.py:39
  21.3 9.9 %collective-permute-start.5 = (bf16[64,1024]{1,0:T(8,128)(2,1)S(1)}, bf16[64,1024]{1,0:T(8,128)(2,1)S(1)}, u32[]{:S(2)}, u32[]{:S(2)}) collective-permute-start(bf16[64,1024]{1,0:T(8,128)(2,1)S(1)} %shard_map.87.summed_ref.refs_0_.basis_ref), channel_id=1, source_target_pairs={{0,128},{1,129},{2,130},{3,131},{4,132},{5,133},{6,134},{7,135},{8... | collective-permute-start | bytes 393224 | tf_op jit(solution)/shard_map/ppermute | solution.py:39
  22.8 8.5 %collective-permute-start.7 = (bf16[64,1024]{1,0:T(8,128)(2,1)S(1)}, bf16[64,1024]{1,0:T(8,128)(2,1)S(1)}, u32[]{:S(2)}, u32[]{:S(2)}) collective-permute-start(bf16[64,1024]{1,0:T(8,128)(2,1)S(1)} %shard_map.87.summed_ref.refs_0_.basis_ref), channel_id=1, source_target_pairs={{0,32},{1,33},{2,34},{3,35},{4,36},{5,37},{6,38},{7,39},{8,40},{9,... | collective-permute-start | bytes 393224 | tf_op jit(solution)/shard_map/ppermute | solution.py:39
  25.1 6.2 %collective-permute-start.10 = (bf16[64,1024]{1,0:T(8,128)(2,1)S(1)}, bf16[64,1024]{1,0:T(8,128)(2,1)S(1)}, u32[]{:S(2)}, u32[]{:S(2)}) collective-permute-start(bf16[64,1024]{1,0:T(8,128)(2,1)S(1)} %collective-permute-done.6.refs_3_), channel_id=1, source_target_pairs={{0,32},{1,33},{2,34},{3,35},{4,36},{5,37},{6,38},{7,39},{8,40},{9,... | collective-permute-start | bytes 393224 | tf_op jit(solution)/shard_map/ppermute | solution.py:39
  36.1 35.6 %collective-permute-start.23 = (bf16[2,128,1024]{2,1,0:T(8,128)(2,1)S(1)}, bf16[2,128,1024]{2,1,0:T(8,128)(2,1)S(1)}, u32[]{:S(2)}, u32[]{:S(2)}) collective-permute-start(bf16[2,128,1024]{2,1,0:T(8,128)(2,1)S(1)} %get-tuple-element.46), channel_id=1, source_target_pairs={{0,64},{1,65},{2,66},{3,67},{4,68},{5,69},{6,70},{7,71},{8,72},{9,... | collective-permute-start | bytes 1572872 | tf_op jit(solution)/shard_map/ppermute | solution.py:39
  36.2 35.5 %collective-permute-start.24 = (bf16[2,128,1024]{2,1,0:T(8,128)(2,1)S(1)}, bf16[2,128,1024]{2,1,0:T(8,128)(2,1)S(1)}, u32[]{:S(2)}, u32[]{:S(2)}) collective-permute-start(bf16[2,128,1024]{2,1,0:T(8,128)(2,1)S(1)} %get-tuple-element.47), channel_id=1, source_target_pairs={{0,128},{1,129},{2,130},{3,131},{4,132},{5,133},{6,134},{7,135},{8... | collective-permute-start | bytes 1572872 | tf_op jit(solution)/shard_map/ppermute | solution.py:39
  38.0 33.7 %collective-permute-start.25 = (bf16[2,128,1024]{2,1,0:T(8,128)(2,1)S(1)}, bf16[2,128,1024]{2,1,0:T(8,128)(2,1)S(1)}, u32[]{:S(2)}, u32[]{:S(2)}) collective-permute-start(bf16[2,128,1024]{2,1,0:T(8,128)(2,1)S(1)} %get-tuple-element.48), channel_id=1, source_target_pairs={{0,192},{1,193},{2,194},{3,195},{4,196},{5,197},{6,198},{7,199},{8... | collective-permute-start | bytes 1572872 | tf_op jit(solution)/shard_map/ppermute | solution.py:39
  38.9 26.2 %collective-permute-start.12 = (bf16[64,1024]{1,0:T(8,128)(2,1)S(1)}, bf16[64,1024]{1,0:T(8,128)(2,1)S(1)}, u32[]{:S(2)}, u32[]{:S(2)}) collective-permute-start(bf16[64,1024]{1,0:T(8,128)(2,1)S(1)} %get-tuple-element.41), channel_id=1, source_target_pairs={{0,64},{1,65},{2,66},{3,67},{4,68},{5,69},{6,70},{7,71},{8,72},{9,... | collective-permute-start | bytes 393224 | tf_op jit(solution)/shard_map/ppermute | solution.py:39
  39.7 31.6 %collective-permute-start.13 = (bf16[64,1024]{1,0:T(8,128)(2,1)S(1)}, bf16[64,1024]{1,0:T(8,128)(2,1)S(1)}, u32[]{:S(2)}, u32[]{:S(2)}) collective-permute-start(bf16[64,1024]{1,0:T(8,128)(2,1)S(1)} %get-tuple-element.42), channel_id=1, source_target_pairs={{0,128},{1,129},{2,130},{3,131},{4,132},{5,133},{6,134},{7,135},{8... | collective-permute-start | bytes 393224 | tf_op jit(solution)/shard_map/ppermute | solution.py:39
  65.2 6.1 %collective-permute-start.14 = (bf16[64,1024]{1,0:T(8,128)(2,1)S(1)}, bf16[64,1024]{1,0:T(8,128)(2,1)S(1)}, u32[]{:S(2)}, u32[]{:S(2)}) collective-permute-start(bf16[64,1024]{1,0:T(8,128)(2,1)S(1)} %get-tuple-element.43), channel_id=1, source_target_pairs={{0,192},{1,193},{2,194},{3,195},{4,196},{5,197},{6,198},{7,199},{8... | collective-permute-start | bytes 393224 | tf_op jit(solution)/shard_map/ppermute | solution.py:39
  76.8 5.2 %collective-permute-start.26 = (bf16[4,128,640]{2,1,0:T(8,128)(2,1)S(1)}, bf16[4,128,640]{2,1,0:T(8,128)(2,1)S(1)}, u32[]{:S(2)}, u32[]{:S(2)}) collective-permute-start(bf16[4,128,640]{2,1,0:T(8,128)(2,1)S(1)} %get-tuple-element.50), channel_id=1, source_target_pairs={{0,32},{1,33},{2,34},{3,35},{4,36},{5,37},{6,38},{7,39},{8,40},{9,... | collective-permute-start | bytes 1966088 | tf_op jit(solution)/shard_map/ppermute | solution.py:39
  82.2 10.8 %collective-permute-start.27 = (bf16[2,128,640]{2,1,0:T(8,128)(2,1)S(1)}, bf16[2,128,640]{2,1,0:T(8,128)(2,1)S(1)}, u32[]{:S(2)}, u32[]{:S(2)}) collective-permute-start(bf16[2,128,640]{2,1,0:T(8,128)(2,1)S(1)} %get-tuple-element.51), channel_id=1, source_target_pairs={{0,1},{1,2},{2,3},{3,0},{4,5},{5,6},{6,7},{7,4},{8,9},{9,10},{10,1... | collective-permute-start | bytes 983048 | tf_op jit(solution)/shard_map/ppermute | solution.py:39
  85.4 17.7 %collective-permute-start.28 = (bf16[2,128,640]{2,1,0:T(8,128)(2,1)S(1)}, bf16[2,128,640]{2,1,0:T(8,128)(2,1)S(1)}, u32[]{:S(2)}, u32[]{:S(2)}) collective-permute-start(bf16[2,128,640]{2,1,0:T(8,128)(2,1)S(1)} %get-tuple-element.52), channel_id=1, source_target_pairs={{0,65},{1,66},{2,67},{3,64},{4,69},{5,70},{6,71},{7,68},{8,73},{9,... | collective-permute-start | bytes 983048 | tf_op jit(solution)/shard_map/ppermute | solution.py:39
  87.0 16.1 %collective-permute-start.29 = (bf16[2,128,640]{2,1,0:T(8,128)(2,1)S(1)}, bf16[2,128,640]{2,1,0:T(8,128)(2,1)S(1)}, u32[]{:S(2)}, u32[]{:S(2)}) collective-permute-start(bf16[2,128,640]{2,1,0:T(8,128)(2,1)S(1)} %get-tuple-element.53), channel_id=1, source_target_pairs={{0,129},{1,130},{2,131},{3,128},{4,133},{5,134},{6,135},{7,132},{8... | collective-permute-start | bytes 983048 | tf_op jit(solution)/shard_map/ppermute | solution.py:39
  87.0 19.8 %collective-permute-start.30 = (bf16[2,128,640]{2,1,0:T(8,128)(2,1)S(1)}, bf16[2,128,640]{2,1,0:T(8,128)(2,1)S(1)}, u32[]{:S(2)}, u32[]{:S(2)}) collective-permute-start(bf16[2,128,640]{2,1,0:T(8,128)(2,1)S(1)} %get-tuple-element.54), channel_id=1, source_target_pairs={{0,193},{1,194},{2,195},{3,192},{4,197},{5,198},{6,199},{7,196},{8... | collective-permute-start | bytes 983048 | tf_op jit(solution)/shard_map/ppermute | solution.py:39
  89.4 29.5 %collective-permute-start.15 = (bf16[64,1024]{1,0:T(8,128)(2,1)S(1)}, bf16[64,1024]{1,0:T(8,128)(2,1)S(1)}, u32[]{:S(2)}, u32[]{:S(2)}) collective-permute-start(bf16[64,1024]{1,0:T(8,128)(2,1)S(1)} %shard_map.91.refs_8_.cross_ref), channel_id=1, source_target_pairs={{0,64},{1,65},{2,66},{3,67},{4,68},{5,69},{6,70},{7,71},{8,72},{9,... | collective-permute-start | bytes 393224 | tf_op jit(solution)/shard_map/ppermute | solution.py:39
  93.0 27.4 %collective-permute-start.16 = (bf16[64,1024]{1,0:T(8,128)(2,1)S(1)}, bf16[64,1024]{1,0:T(8,128)(2,1)S(1)}, u32[]{:S(2)}, u32[]{:S(2)}) collective-permute-start(bf16[64,1024]{1,0:T(8,128)(2,1)S(1)} %shard_map.91.refs_8_.cross_ref), channel_id=1, source_target_pairs={{0,128},{1,129},{2,130},{3,131},{4,132},{5,133},{6,134},{7,135},{8... | collective-permute-start | bytes 393224 | tf_op jit(solution)/shard_map/ppermute | solution.py:39
  107.2 13.6 %collective-permute-start.31 = (bf16[128,640]{1,0:T(8,128)(2,1)S(1)}, bf16[128,640]{1,0:T(8,128)(2,1)S(1)}, u32[]{:S(2)}, u32[]{:S(2)}) collective-permute-start(bf16[128,640]{1,0:T(8,128)(2,1)S(1)} %get-tuple-element.56), channel_id=1, source_target_pairs={{0,4},{1,5},{2,6},{3,7},{4,8},{5,9},{6,10},{7,11},{8,12},{9,13},{1... | collective-permute-start | bytes 491528 | tf_op jit(solution)/shard_map/ppermute | solution.py:39
  108.9 11.5 %collective-permute-start.17 = (bf16[64,1024]{1,0:T(8,128)(2,1)S(1)}, bf16[64,1024]{1,0:T(8,128)(2,1)S(1)}, u32[]{:S(2)}, u32[]{:S(2)}) collective-permute-start(bf16[64,1024]{1,0:T(8,128)(2,1)S(1)} %shard_map.91.refs_8_.cross_ref), channel_id=1, source_target_pairs={{0,192},{1,193},{2,194},{3,195},{4,196},{5,197},{6,198},{7,199},{8... | collective-permute-start | bytes 393224 | tf_op jit(solution)/shard_map/ppermute | solution.py:39
  114.8 10.5 %collective-permute-start.32 = (bf16[128,640]{1,0:T(8,128)(2,1)S(1)}, bf16[128,640]{1,0:T(8,128)(2,1)S(1)}, u32[]{:S(2)}, u32[]{:S(2)}) collective-permute-start(bf16[128,640]{1,0:T(8,128)(2,1)S(1)} %get-tuple-element.57), channel_id=1, source_target_pairs={{0,8},{1,9},{2,10},{3,11},{4,12},{5,13},{6,14},{7,15},{8,16},{9,17... | collective-permute-start | bytes 491528 | tf_op jit(solution)/shard_map/ppermute | solution.py:39
  119.0 8.2 %collective-permute-start.18 = (bf16[64,1024]{1,0:T(8,128)(2,1)S(1)}, bf16[64,1024]{1,0:T(8,128)(2,1)S(1)}, u32[]{:S(2)}, u32[]{:S(2)}) collective-permute-start(bf16[64,1024]{1,0:T(8,128)(2,1)S(1)} %shard_map.91.refs_8_.cross_ref), channel_id=1, source_target_pairs={{0,32},{1,33},{2,34},{3,35},{4,36},{5,37},{6,38},{7,39},{8,40},{9,... | collective-permute-start | bytes 393224 | tf_op jit(solution)/shard_map/ppermute | solution.py:39
  120.3 10.3 %collective-permute-start.19 = (bf16[64,1024]{1,0:T(8,128)(2,1)S(1)}, bf16[64,1024]{1,0:T(8,128)(2,1)S(1)}, u32[]{:S(2)}, u32[]{:S(2)}) collective-permute-start(bf16[64,1024]{1,0:T(8,128)(2,1)S(1)} %collective-permute-done.15.refs_9_), channel_id=1, source_target_pairs={{0,32},{1,33},{2,34},{3,35},{4,36},{5,37},{6,38},{7,39},{8,40},{9,... | collective-permute-start | bytes 393224 | tf_op jit(solution)/shard_map/ppermute | solution.py:39
  120.4 10.3 %collective-permute-start.20 = (bf16[64,1024]{1,0:T(8,128)(2,1)S(1)}, bf16[64,1024]{1,0:T(8,128)(2,1)S(1)}, u32[]{:S(2)}, u32[]{:S(2)}) collective-permute-start(bf16[64,1024]{1,0:T(8,128)(2,1)S(1)} %collective-permute-done.16.refs_10_), channel_id=1, source_target_pairs={{0,32},{1,33},{2,34},{3,35},{4,36},{5,37},{6,38},{7,39},{8,40},{9,... | collective-permute-start | bytes 393224 | tf_op jit(solution)/shard_map/ppermute | solution.py:39
  120.8 9.9 %collective-permute-start.21 = (bf16[64,1024]{1,0:T(8,128)(2,1)S(1)}, bf16[64,1024]{1,0:T(8,128)(2,1)S(1)}, u32[]{:S(2)}, u32[]{:S(2)}) collective-permute-start(bf16[64,1024]{1,0:T(8,128)(2,1)S(1)} %collective-permute-done.17.refs_11_), channel_id=1, source_target_pairs={{0,32},{1,33},{2,34},{3,35},{4,36},{5,37},{6,38},{7,39},{8,40},{9,... | collective-permute-start | bytes 393224 | tf_op jit(solution)/shard_map/ppermute | solution.py:39
  125.4 9.3 %collective-permute-start.33 = (f32[128,128]{1,0:T(8,128)S(1)}, f32[128,128]{1,0:T(8,128)S(1)}, u32[]{:S(2)}, u32[]{:S(2)}) collective-permute-start(f32[128,128]{1,0:T(8,128)S(1)} %get-tuple-element.59), channel_id=1, source_target_pairs={{0,224},{1,225},{2,226},{3,227},{4,228},{5,229},{6,230},{7,231},{8... | collective-permute-start | bytes 196616 | tf_op jit(solution)/shard_map/ppermute | solution.py:39
  127.2 7.6 %collective-permute-start.34 = (f32[128,128]{1,0:T(8,128)S(1)}, f32[128,128]{1,0:T(8,128)S(1)}, u32[]{:S(2)}, u32[]{:S(2)}) collective-permute-start(f32[128,128]{1,0:T(8,128)S(1)} %get-tuple-element.60), channel_id=1, source_target_pairs={{0,192},{1,193},{2,194},{3,195},{4,196},{5,197},{6,198},{7,199},{8... | collective-permute-start | bytes 196616 | tf_op jit(solution)/shard_map/ppermute | solution.py:39
  130.6 5.2 %collective-permute-start.35 = (f32[128,128]{1,0:T(8,128)S(1)}, f32[128,128]{1,0:T(8,128)S(1)}, u32[]{:S(2)}, u32[]{:S(2)}) collective-permute-start(f32[128,128]{1,0:T(8,128)S(1)} %get-tuple-element.61), channel_id=1, source_target_pairs={{0,160},{1,161},{2,162},{3,163},{4,164},{5,165},{6,166},{7,167},{8... | collective-permute-start | bytes 196616 | tf_op jit(solution)/shard_map/ppermute | solution.py:39
  (11 other events, 132.5 us)
where the time goes:
time: 137 us
  waiting for transfers between devices  57.9 us (42%)
  starting transfers between devices  51 us (37%)
  Pallas kernels  26.2 us (19%)
    ppermute x36, waiting for transfers between devices, perm(): return lax.ppermute(block, AXES, pairs)  57.9 us
    ppermute x36, starting transfers between devices, perm(): return lax.ppermute(block, AXES, pairs)  51 us
    pallas_call x13, Pallas kernels, call(): pl.pallas_call(kernel, out_shape=shapes, in_specs=[pl.BlockSpec(memory_sp...  19.9 us
    pallas_call x1, Pallas kernels, sketch_call(): pl.pallas_call(sketch_kernel, out_shape=[pltpu.VMEM(out, BF16), pltpu.VME...  5.44 us
  transfers between devices with their start and end apart: 36, of which 13 were waited for; matrix products, arithmetic and copies ran while one was open for 0% of the time, Pallas kernels for 11%

commit v1 on v0

--- a/solution.py
+++ b/solution.py
@@ -12,6 +12,7 @@
 NU = 8
 NX = 4
 NY = 4
+NZ = 8
 NC = 32
 HALF = 5
 BLK = 128
@@ -51,8 +52,13 @@
     return (u ^ 1, c)
 
 
-def to_column(k):
-    return lambda u, c: ((u + 2 * k) % NU, c // NY * NY + (c + u // 2 + 1) % NY)
+def to_column(k, other):
+    def route(u, c):
+        x, core = u // 2, u % 2
+        plane, y = c // NY, c % NY
+        return (2 * ((x + k) % NX) + (core ^ other), (plane + core) % NZ * NY + (y + x + 1) % NY)
+
+    return route
 
 
 def along_z(k):
@@ -229,7 +235,8 @@
     return call(split_kernel, [shape] * 2, [panel])
 
 
-def tile_kernel(basis_ref, cross_ref, dinv_ref, keep_ref, got_ref, a_ref, b_ref, c_ref, send_out, keep_out, updated, solved):
+def tile_kernel(basis_ref, cross_ref, dinv_ref, keep_ref, got_ref, a_ref, b_ref, c_ref, *refs):
+    outs, (updated, solved) = refs[:NU], refs[NU:]
     x, core = place()
     lowrank = dot(basis_ref[...], cross_ref[...], LEFT)
     updated[...] = lowrank
@@ -251,16 +258,16 @@
         upper = product[:BLK, : HALF * BLK].astype(BF16)
         lower = product[BLK:, BLK:].astype(BF16)
         on_lower = core == 1
-        keep_out[k] = jnp.where(on_lower, lower, upper)
-        send_out[k] = jnp.where(on_lower, upper, lower)
+        outs[2 * k][...] = jnp.where(on_lower, lower, upper)
+        outs[2 * k + 1][...] = jnp.where(on_lower, upper, lower)
 
 
 def tile_call(basis, cross, dinv, rows):
     width = dinv.shape[0]
-    out = ((NX, BLK, HALF * BLK), BF16)
+    out = ((BLK, HALF * BLK), BF16)
     return call(
         tile_kernel,
-        [out, out],
+        [out] * NU,
         [basis, cross, dinv, *rows],
         scratch=[
             pltpu.VMEM((width, width), F32),
@@ -308,30 +315,32 @@
     )[0]
 
 
-def arrived_kernel(a_ref, b_ref, c_ref, d_ref, here_ref, one_ref, two_ref):
-    x, core = place()
-    y = lax.axis_index("col") & 3
-    here = one = two = None
-    for k, ref in enumerate((a_ref, b_ref, c_ref, d_ref)):
+def arrived_kernel(*refs):
+    refs, (here_ref, onward_ref) = refs[:NU], refs[NU:]
+    x, core = place()
+    col = lax.axis_index("col")
+    y, z = col & 3, col >> 2
+    here, onward = 0.0, 0.0
+    for k in range(NX):
+        first, second = refs[2 * k][...].astype(F32), refs[2 * k + 1][...].astype(F32)
+        near = jnp.where(core == 0, first, second)
+        far = jnp.where(core == 0, second, first)
+        both = near + jnp.where(z > 0, far, 0.0)
         stays = y > ((x - k) & 3)
-        near, far = ref[core].astype(F32), ref[core ^ 1].astype(F32)
-        parts = (jnp.where(stays, near, 0.0), jnp.where(stays, far, near), jnp.where(stays, 0.0, far))
-        here, one, two = parts if k == 0 else (here + parts[0], one + parts[1], two + parts[2])
+        here = here + jnp.where(stays, both, 0.0)
+        onward = onward + jnp.where(stays, 0.0, both)
     here_ref[...] = here
-    one_ref[...] = one.astype(BF16)
-    two_ref[...] = two.astype(BF16)
+    onward_ref[...] = onward.astype(BF16)
 
 
 def arrived_sum(arrived):
-    shape = arrived[0].shape[1:]
-    outs = [(shape, F32), (shape, BF16), (shape, BF16)]
-    return call(arrived_kernel, outs, arrived)
-
-
-def collect_kernel(here_ref, one_ref, two_ref, total_ref, a_ref, b_ref, c_ref):
+    shape = arrived[0].shape
+    return call(arrived_kernel, [(shape, F32), (shape, BF16)], arrived)
+
+
+def collect_kernel(here_ref, onward_ref, total_ref, a_ref, b_ref, c_ref):
     z = lax.axis_index("col") >> 2
-    total = here_ref[...] + jnp.where(z >= 1, one_ref[...].astype(F32), 0.0)
-    total = total + jnp.where(z >= 2, two_ref[...].astype(F32), 0.0)
+    total = here_ref[...] + jnp.where(z > 0, onward_ref[...].astype(F32), 0.0)
     total_ref[...] = total
     for d, ref in ((1, a_ref), (2, b_ref), (3, c_ref)):
         i = HALF - 1 - d
@@ -398,13 +407,11 @@
     own, *others = pair_sum(keep, got)
     others = shifted(others, along_x)
     cross = cross_total(inverse, own, others)
-    send, keep = tile_call(own_sum, cross, dinv, rows)
-    got = perm(send, partner)
-    blocks = bundles(keep, got, 0)
-    arrived = shifted(blocks, to_column, 0)
+    blocks = tile_call(own_sum, cross, dinv, rows)
+    arrived = shifted(blocks, lambda i: to_column(i // 2, i % 2), 0)
     crosses = gathered(cross)
-    here, *onward = arrived_sum(arrived)
-    onward = shifted(onward, along_z)
+    here, onward = arrived_sum(arrived)
+    onward = [perm(onward, along_z(1))]
     total, *mirrored = collect(here, onward)
     mirrored = shifted(mirrored, lambda d: along_upd(-d))
     panel_out = rows_call(panel, dinv, sums, crosses)

time: 137 us -> 134 us (0.978)
  the two profiles are of different devices: /device:TPU:41 before, /device:TPU:1 now
where the time goes in v1:
time: 134 us
  starting transfers between devices  55 us (41%)
  waiting for transfers between devices  50.9 us (38%)
  Pallas kernels  26.1 us (19%)
    ppermute x38, starting transfers between devices, perm(): return lax.ppermute(block, AXES, pairs)  55 us
    ppermute x38, waiting for transfers between devices, perm(): return lax.ppermute(block, AXES, pairs)  50.9 us
    pallas_call x12, Pallas kernels, call(): pl.pallas_call(kernel, out_shape=shapes, in_specs=[pl.BlockSpec(memory_sp...  19.8 us
    pallas_call x1, Pallas kernels, sketch_call(): pl.pallas_call(sketch_kernel, out_shape=[pltpu.VMEM(out, BF16), pltpu.VME...  5.43 us
  transfers between devices with their start and end apart: 38, of which 12 were waited for; matrix products, arithmetic and copies ran while one was open for 0% of the time, Pallas kernels for 11%

profile of v1, /device:TPU:1, one launch (start us, length us, event | category | flops | bytes accessed | tf_op | source)
XLA Modules:
  0.0 133.8 jit_solution(9100463816612025256)
XLA Ops:
  1.4 5.4 %sketch_product.1 = (bf16[4,64,1024]{2,1,0:T(8,128)(2,1)S(1)}, f32[4,64,1024]{2,1,0:T(8,128)S(1)}) custom-call(s32[8]{0:T(128)S(1)} %bitcast.18, bf16[8,96,1024]{2,1,0:T(8,128)(2,1)} %bitcast.13, bf16[8,96,1024]{2,1,0:T(8,128)(2,1)} %bitcast.15, bf16[64,1024]{1,0:T(8,128)(2,1)} %bitcast.22), custom_call_target="tpu_custom_call" | custom-call | tf_op jit(solution)/shard_map/sketch_product/pallas_call | solution.py:121
  6.9 3.3 %collective-permute-start = (bf16[4,64,1024]{2,1,0:T(8,128)(2,1)S(1)}, bf16[4,64,1024]{2,1,0:T(8,128)(2,1)S(1)}, u32[]{:S(2)}, u32[]{:S(2)}) collective-permute-start(bf16[4,64,1024]{2,1,0:T(8,128)(2,1)S(1)} %get-tuple-element.34), channel_id=1, source_target_pairs={{0,32},{1,33},{2,34},{3,35},{4,36},{5,37},{6,38},{7,39},{8,40},{9,... | collective-permute-start | bytes 1572872 | tf_op jit(solution)/shard_map/ppermute | solution.py:40
  10.5 1.2 collective-permute-done.got_ref
  11.9 1.9 %collective-permute-start.2 = (bf16[64,1024]{1,0:T(8,128)(2,1)S(1)}, bf16[64,1024]{1,0:T(8,128)(2,1)S(1)}, u32[]{:S(2)}, u32[]{:S(2)}) collective-permute-start(bf16[64,1024]{1,0:T(8,128)(2,1)S(1)} %get-tuple-element.37), channel_id=1, source_target_pairs={{0,128},{1,129},{2,130},{3,131},{4,132},{5,133},{6,134},{7,135},{8... | collective-permute-start | bytes 393224 | tf_op jit(solution)/shard_map/ppermute | solution.py:40
  13.8 1.2 collective-permute-start.3
  15.0 3.5 %collective-permute-done.1.a_ref = bf16[64,1024]{1,0:T(8,128)(2,1)S(1)} collective-permute-done((bf16[64,1024]{1,0:T(8,128)(2,1)S(1)}, bf16[64,1024]{1,0:T(8,128)(2,1)S(1)}, u32[]{:S(2)}, u32[]{:S(2)}) %collective-permute-start.1) | collective-permute-done | bytes 131104 | tf_op jit(solution)/shard_map/ppermute | solution.py:40
  18.5 1.4 %collective-permute-done.2.b_ref = bf16[64,1024]{1,0:T(8,128)(2,1)S(1)} collective-permute-done((bf16[64,1024]{1,0:T(8,128)(2,1)S(1)}, bf16[64,1024]{1,0:T(8,128)(2,1)S(1)}, u32[]{:S(2)}, u32[]{:S(2)}) %collective-permute-start.2) | collective-permute-done | bytes 131104 | tf_op jit(solution)/shard_map/ppermute | solution.py:40
  21.0 3.5 %collective-permute-start.6 = (bf16[64,1024]{1,0:T(8,128)(2,1)S(1)}, bf16[64,1024]{1,0:T(8,128)(2,1)S(1)}, u32[]{:S(2)}, u32[]{:S(2)}) collective-permute-start(bf16[64,1024]{1,0:T(8,128)(2,1)S(1)} %shard_map.87.summed_ref.refs_0_.basis_ref), channel_id=1, source_target_pairs={{0,192},{1,193},{2,194},{3,195},{4,196},{5,197},{6,198},{7,199},{8... | collective-permute-start | bytes 393224 | tf_op jit(solution)/shard_map/ppermute | solution.py:40
  24.4 1.3 collective-permute-start.5
  26.8 1.3 %collective-permute-start.10 = (bf16[64,1024]{1,0:T(8,128)(2,1)S(1)}, bf16[64,1024]{1,0:T(8,128)(2,1)S(1)}, u32[]{:S(2)}, u32[]{:S(2)}) collective-permute-start(bf16[64,1024]{1,0:T(8,128)(2,1)S(1)} %collective-permute-done.6.refs_3_), channel_id=1, source_target_pairs={{0,32},{1,33},{2,34},{3,35},{4,36},{5,37},{6,38},{7,39},{8,40},{9,... | collective-permute-start | bytes 393224 | tf_op jit(solution)/shard_map/ppermute | solution.py:40
  28.1 5.0 %collective-permute-done.4.refs_1_ = bf16[64,1024]{1,0:T(8,128)(2,1)S(1)} collective-permute-done((bf16[64,1024]{1,0:T(8,128)(2,1)S(1)}, bf16[64,1024]{1,0:T(8,128)(2,1)S(1)}, u32[]{:S(2)}, u32[]{:S(2)}) %collective-permute-start.4) | collective-permute-done | bytes 131104 | tf_op jit(solution)/shard_map/ppermute | solution.py:40
  33.1 1.2 collective-permute-start.8
  35.7 3.1 %shard_map.89 = (bf16[4,64,1024]{2,1,0:T(8,128)(2,1)S(1)}, f32[4,64,1024]{2,1,0:T(8,128)S(1)}) custom-call(s32[8]{0:T(128)S(1)} %bitcast.19, bf16[8,96,1024]{2,1,0:T(8,128)(2,1)S(1)} %bitcast.16, bf16[8,96,1024]{2,1,0:T(8,128)(2,1)S(1)} %bitcast.14, bf16[64,1024]{1,0:T(8,128)(2,1)S(1)} %shard_map.87.summed_ref.refs_0_.basis_ref, ...), custom_call_target="tpu_custom_call" | custom-call | tf_op jit(solution)/shard_map/pallas_call | solution.py:75
  39.3 1.3 collective-permute-start.24
  40.5 1.4 %collective-permute-start.25 = (bf16[2,128,1024]{2,1,0:T(8,128)(2,1)S(1)}, bf16[2,128,1024]{2,1,0:T(8,128)(2,1)S(1)}, u32[]{:S(2)}, u32[]{:S(2)}) collective-permute-start(bf16[2,128,1024]{2,1,0:T(8,128)(2,1)S(1)} %get-tuple-element.49), channel_id=1, source_target_pairs={{0,192},{1,193},{2,194},{3,195},{4,196},{5,197},{6,198},{7,199},{8... | collective-permute-start | bytes 1572872 | tf_op jit(solution)/shard_map/ppermute | solution.py:40
  42.7 1.9 %collective-permute-start.13 = (bf16[64,1024]{1,0:T(8,128)(2,1)S(1)}, bf16[64,1024]{1,0:T(8,128)(2,1)S(1)}, u32[]{:S(2)}, u32[]{:S(2)}) collective-permute-start(bf16[64,1024]{1,0:T(8,128)(2,1)S(1)} %get-tuple-element.43), channel_id=1, source_target_pairs={{0,128},{1,129},{2,130},{3,131},{4,132},{5,133},{6,134},{7,135},{8... | collective-permute-start | bytes 393224 | tf_op jit(solution)/shard_map/ppermute | solution.py:40
  44.6 25.9 %collective-permute-done.12.a_ref = bf16[64,1024]{1,0:T(8,128)(2,1)S(1)} collective-permute-done((bf16[64,1024]{1,0:T(8,128)(2,1)S(1)}, bf16[64,1024]{1,0:T(8,128)(2,1)S(1)}, u32[]{:S(2)}, u32[]{:S(2)}) %collective-permute-start.12) | collective-permute-done | bytes 131104 | tf_op jit(solution)/shard_map/ppermute | solution.py:40
  70.5 6.1 %shard_map.88.inverse_ref = f32[64,64]{1,0:T(8,128)S(1)} custom-call(bf16[64,1024]{1,0:T(8,128)(2,1)S(1)} %shard_map.87.summed_ref.refs_0_.basis_ref), custom_call_target="tpu_custom_call" | custom-call | tf_op jit(solution)/shard_map/pallas_call | solution.py:75
  77.0 5.2 %shard_map.95 = (bf16[128,640]{1,0:T(8,128)(2,1)S(1)}, bf16[128,640]{1,0:T(8,128)(2,1)S(1)}, bf16[128,640]{1,0:T(8,128)(2,1)S(1)}, bf16[128,640]{1,0:T(8,128)(2,...) custom-call(bf16[64,1024]{1,0:T(8,128)(2,1)S(1)} %shard_map.87.summe, ...), custom_call_target="tpu_custom_call" | custom-call | tf_op jit(solution)/shard_map/pallas_call | solution.py:75
  82.2 1.9 %collective-permute-start.26 = (bf16[128,640]{1,0:T(8,128)(2,1)S(1)}, bf16[128,640]{1,0:T(8,128)(2,1)S(1)}, u32[]{:S(2)}, u32[]{:S(2)}) collective-permute-start(bf16[128,640]{1,0:T(8,128)(2,1)S(1)} %get-tuple-element.50), channel_id=1, source_target_pairs={{0,1},{1,2},{2,3},{3,0},{4,5},{5,6},{6,7},{7,4},{8,9},{9,10},{10,1... | collective-permute-start | bytes 491528 | tf_op jit(solution)/shard_map/ppermute | solution.py:40
  84.1 3.1 %collective-permute-start.27 = (bf16[128,640]{1,0:T(8,128)(2,1)S(1)}, bf16[128,640]{1,0:T(8,128)(2,1)S(1)}, u32[]{:S(2)}, u32[]{:S(2)}) collective-permute-start(bf16[128,640]{1,0:T(8,128)(2,1)S(1)} %get-tuple-element.51), channel_id=1, source_target_pairs={{0,33},{1,34},{2,35},{3,32},{4,37},{5,38},{6,39},{7,36},{8,41},{9,... | collective-permute-start | bytes 491528 | tf_op jit(solution)/shard_map/ppermute | solution.py:40
  87.2 4.5 %collective-permute-start.28 = (bf16[128,640]{1,0:T(8,128)(2,1)S(1)}, bf16[128,640]{1,0:T(8,128)(2,1)S(1)}, u32[]{:S(2)}, u32[]{:S(2)}) collective-permute-start(bf16[128,640]{1,0:T(8,128)(2,1)S(1)} %get-tuple-element.52), channel_id=1, source_target_pairs={{0,65},{1,66},{2,67},{3,64},{4,69},{5,70},{6,71},{7,68},{8,73},{9,... | collective-permute-start | bytes 491528 | tf_op jit(solution)/shard_map/ppermute | solution.py:40
  92.4 3.7 %collective-permute-start.31 = (bf16[128,640]{1,0:T(8,128)(2,1)S(1)}, bf16[128,640]{1,0:T(8,128)(2,1)S(1)}, u32[]{:S(2)}, u32[]{:S(2)}) collective-permute-start(bf16[128,640]{1,0:T(8,128)(2,1)S(1)} %get-tuple-element.55), channel_id=1, source_target_pairs={{0,161},{1,162},{2,163},{3,160},{4,165},{5,166},{6,167},{7,164},{8... | collective-permute-start | bytes 491528 | tf_op jit(solution)/shard_map/ppermute | solution.py:40
  96.7 6.5 %collective-permute-start.32 = (bf16[128,640]{1,0:T(8,128)(2,1)S(1)}, bf16[128,640]{1,0:T(8,128)(2,1)S(1)}, u32[]{:S(2)}, u32[]{:S(2)}) collective-permute-start(bf16[128,640]{1,0:T(8,128)(2,1)S(1)} %get-tuple-element.56), channel_id=1, source_target_pairs={{0,193},{1,194},{2,195},{3,192},{4,197},{5,198},{6,199},{7,196},{8... | collective-permute-start | bytes 491528 | tf_op jit(solution)/shard_map/ppermute | solution.py:40
  103.2 2.8 %collective-permute-start.15 = (bf16[64,1024]{1,0:T(8,128)(2,1)S(1)}, bf16[64,1024]{1,0:T(8,128)(2,1)S(1)}, u32[]{:S(2)}, u32[]{:S(2)}) collective-permute-start(bf16[64,1024]{1,0:T(8,128)(2,1)S(1)} %shard_map.91.refs_8_.cross_ref), channel_id=1, source_target_pairs={{0,64},{1,65},{2,66},{3,67},{4,68},{5,69},{6,70},{7,71},{8,72},{9,... | collective-permute-start | bytes 393224 | tf_op jit(solution)/shard_map/ppermute | solution.py:40
  106.5 3.6 %collective-permute-start.17 = (bf16[64,1024]{1,0:T(8,128)(2,1)S(1)}, bf16[64,1024]{1,0:T(8,128)(2,1)S(1)}, u32[]{:S(2)}, u32[]{:S(2)}) collective-permute-start(bf16[64,1024]{1,0:T(8,128)(2,1)S(1)} %shard_map.91.refs_8_.cross_ref), channel_id=1, source_target_pairs={{0,192},{1,193},{2,194},{3,195},{4,196},{5,197},{6,198},{7,199},{8... | collective-permute-start | bytes 393224 | tf_op jit(solution)/shard_map/ppermute | solution.py:40
  110.2 5.1 %collective-permute-done.33.refs_7_ = bf16[128,640]{1,0:T(8,128)(2,1)S(1)} collective-permute-done((bf16[128,640]{1,0:T(8,128)(2,1)S(1)}, bf16[128,640]{1,0:T(8,128)(2,1)S(1)}, u32[]{:S(2)}, u32[]{:S(2)}) %collective-permute-start.33) | collective-permute-done | bytes 163872 | tf_op jit(solution)/shard_map/ppermute | solution.py:40
  117.1 2.7 %collective-permute-start.21 = (bf16[64,1024]{1,0:T(8,128)(2,1)S(1)}, bf16[64,1024]{1,0:T(8,128)(2,1)S(1)}, u32[]{:S(2)}, u32[]{:S(2)}) collective-permute-start(bf16[64,1024]{1,0:T(8,128)(2,1)S(1)} %collective-permute-done.17.refs_11_), channel_id=1, source_target_pairs={{0,32},{1,33},{2,34},{3,35},{4,36},{5,37},{6,38},{7,39},{8,40},{9,... | collective-permute-start | bytes 393224 | tf_op jit(solution)/shard_map/ppermute | solution.py:40
  119.8 4.8 %collective-permute-done.34.onward_ref = bf16[128,640]{1,0:T(8,128)(2,1)S(1)} collective-permute-done((bf16[128,640]{1,0:T(8,128)(2,1)S(1)}, bf16[128,640]{1,0:T(8,128)(2,1)S(1)}, u32[]{:S(2)}, u32[]{:S(2)}) %collective-permute-start.34) | collective-permute-done | bytes 163872 | tf_op jit(solution)/shard_map/ppermute | solution.py:40
  124.7 2.9 %collective-permute-start.36 = (f32[128,128]{1,0:T(8,128)S(1)}, f32[128,128]{1,0:T(8,128)S(1)}, u32[]{:S(2)}, u32[]{:S(2)}) collective-permute-start(f32[128,128]{1,0:T(8,128)S(1)} %get-tuple-element.62), channel_id=1, source_target_pairs={{0,192},{1,193},{2,194},{3,195},{4,196},{5,197},{6,198},{7,199},{8... | collective-permute-start | bytes 196616 | tf_op jit(solution)/shard_map/ppermute | solution.py:40
  127.7 4.0 %shard_map.92 = bf16[8,128,1024]{2,1,0:T(8,128)(2,1)} custom-call(bf16[8,128,1024]{2,1,0:T(8,128)(2,1)S(1)} %bitcast.12, bf16[1024,1024]{1,0:T(8,128)(2,1)S(1)} %bitcast.10, bf16[64,1024]{1,0:T(8,128)(2,1)S(1)} %shard_map.87.summed_ref.refs_0_.basis_ref, bf16[64,1024]{1,0:T(8,128)(2,1)S(1)} %collective-permute-done.4.refs_1_, ...), custom_call_target="tpu_custom_call" | custom-call | tf_op jit(solution)/shard_map/pallas_call | solution.py:75
  131.7 1.1 collective-permute-done.37.c_ref
  (72 shorter events, 11.0 us)
Async XLA Ops:
  10.3 28.7 %collective-permute-start.22 = (bf16[4,128,1024]{2,1,0:T(8,128)(2,1)S(1)}, bf16[4,128,1024]{2,1,0:T(8,128)(2,1)S(1)}, u32[]{:S(2)}, u32[]{:S(2)}) collective-permute-start(bf16[4,128,1024]{2,1,0:T(8,128)(2,1)S(1)} %get-tuple-element.46), channel_id=1, source_target_pairs={{0,32},{1,33},{2,34},{3,35},{4,36},{5,37},{6,38},{7,39},{8,40},{9,... | collective-permute-start | bytes 3145736 | tf_op jit(solution)/shard_map/ppermute | solution.py:40
  11.8 6.7 %collective-permute-start.1 = (bf16[64,1024]{1,0:T(8,128)(2,1)S(1)}, bf16[64,1024]{1,0:T(8,128)(2,1)S(1)}, u32[]{:S(2)}, u32[]{:S(2)}) collective-permute-start(bf16[64,1024]{1,0:T(8,128)(2,1)S(1)} %get-tuple-element.36), channel_id=1, source_target_pairs={{0,64},{1,65},{2,66},{3,67},{4,68},{5,69},{6,70},{7,71},{8,72},{9,... | collective-permute-start | bytes 393224 | tf_op jit(solution)/shard_map/ppermute | solution.py:40
  11.9 8.0 %collective-permute-start.2 = (bf16[64,1024]{1,0:T(8,128)(2,1)S(1)}, bf16[64,1024]{1,0:T(8,128)(2,1)S(1)}, u32[]{:S(2)}, u32[]{:S(2)}) collective-permute-start(bf16[64,1024]{1,0:T(8,128)(2,1)S(1)} %get-tuple-element.37), channel_id=1, source_target_pairs={{0,128},{1,129},{2,130},{3,131},{4,132},{5,133},{6,134},{7,135},{8... | collective-permute-start | bytes 393224 | tf_op jit(solution)/shard_map/ppermute | solution.py:40
  13.8 7.0 %collective-permute-start.3 = (bf16[64,1024]{1,0:T(8,128)(2,1)S(1)}, bf16[64,1024]{1,0:T(8,128)(2,1)S(1)}, u32[]{:S(2)}, u32[]{:S(2)}) collective-permute-start(bf16[64,1024]{1,0:T(8,128)(2,1)S(1)} %get-tuple-element.38), channel_id=1, source_target_pairs={{0,192},{1,193},{2,194},{3,195},{4,196},{5,197},{6,198},{7,199},{8... | collective-permute-start | bytes 393224 | tf_op jit(solution)/shard_map/ppermute | solution.py:40
  24.4 8.7 %collective-permute-start.4 = (bf16[64,1024]{1,0:T(8,128)(2,1)S(1)}, bf16[64,1024]{1,0:T(8,128)(2,1)S(1)}, u32[]{:S(2)}, u32[]{:S(2)}) collective-permute-start(bf16[64,1024]{1,0:T(8,128)(2,1)S(1)} %shard_map.87.summed_ref.refs_0_.basis_ref), channel_id=1, source_target_pairs={{0,64},{1,65},{2,66},{3,67},{4,68},{5,69},{6,70},{7,71},{8,72},{9,... | collective-permute-start | bytes 393224 | tf_op jit(solution)/shard_map/ppermute | solution.py:40
  24.4 9.9 %collective-permute-start.5 = (bf16[64,1024]{1,0:T(8,128)(2,1)S(1)}, bf16[64,1024]{1,0:T(8,128)(2,1)S(1)}, u32[]{:S(2)}, u32[]{:S(2)}) collective-permute-start(bf16[64,1024]{1,0:T(8,128)(2,1)S(1)} %shard_map.87.summed_ref.refs_0_.basis_ref), channel_id=1, source_target_pairs={{0,128},{1,129},{2,130},{3,131},{4,132},{5,133},{6,134},{7,135},{8... | collective-permute-start | bytes 393224 | tf_op jit(solution)/shard_map/ppermute | solution.py:40
  25.7 8.7 %collective-permute-start.7 = (bf16[64,1024]{1,0:T(8,128)(2,1)S(1)}, bf16[64,1024]{1,0:T(8,128)(2,1)S(1)}, u32[]{:S(2)}, u32[]{:S(2)}) collective-permute-start(bf16[64,1024]{1,0:T(8,128)(2,1)S(1)} %shard_map.87.summed_ref.refs_0_.basis_ref), channel_id=1, source_target_pairs={{0,32},{1,33},{2,34},{3,35},{4,36},{5,37},{6,38},{7,39},{8,40},{9,... | collective-permute-start | bytes 393224 | tf_op jit(solution)/shard_map/ppermute | solution.py:40
  26.8 7.6 %collective-permute-start.10 = (bf16[64,1024]{1,0:T(8,128)(2,1)S(1)}, bf16[64,1024]{1,0:T(8,128)(2,1)S(1)}, u32[]{:S(2)}, u32[]{:S(2)}) collective-permute-start(bf16[64,1024]{1,0:T(8,128)(2,1)S(1)} %collective-permute-done.6.refs_3_), channel_id=1, source_target_pairs={{0,32},{1,33},{2,34},{3,35},{4,36},{5,37},{6,38},{7,39},{8,40},{9,... | collective-permute-start | bytes 393224 | tf_op jit(solution)/shard_map/ppermute | solution.py:40
  39.2 37.8 %collective-permute-start.23 = (bf16[2,128,1024]{2,1,0:T(8,128)(2,1)S(1)}, bf16[2,128,1024]{2,1,0:T(8,128)(2,1)S(1)}, u32[]{:S(2)}, u32[]{:S(2)}) collective-permute-start(bf16[2,128,1024]{2,1,0:T(8,128)(2,1)S(1)} %get-tuple-element.47), channel_id=1, source_target_pairs={{0,64},{1,65},{2,66},{3,67},{4,68},{5,69},{6,70},{7,71},{8,72},{9,... | collective-permute-start | bytes 1572872 | tf_op jit(solution)/shard_map/ppermute | solution.py:40
  39.3 37.7 %collective-permute-start.24 = (bf16[2,128,1024]{2,1,0:T(8,128)(2,1)S(1)}, bf16[2,128,1024]{2,1,0:T(8,128)(2,1)S(1)}, u32[]{:S(2)}, u32[]{:S(2)}) collective-permute-start(bf16[2,128,1024]{2,1,0:T(8,128)(2,1)S(1)} %get-tuple-element.48), channel_id=1, source_target_pairs={{0,128},{1,129},{2,130},{3,131},{4,132},{5,133},{6,134},{7,135},{8... | collective-permute-start | bytes 1572872 | tf_op jit(solution)/shard_map/ppermute | solution.py:40
  40.5 36.5 %collective-permute-start.25 = (bf16[2,128,1024]{2,1,0:T(8,128)(2,1)S(1)}, bf16[2,128,1024]{2,1,0:T(8,128)(2,1)S(1)}, u32[]{:S(2)}, u32[]{:S(2)}) collective-permute-start(bf16[2,128,1024]{2,1,0:T(8,128)(2,1)S(1)} %get-tuple-element.49), channel_id=1, source_target_pairs={{0,192},{1,193},{2,194},{3,195},{4,196},{5,197},{6,198},{7,199},{8... | collective-permute-start | bytes 1572872 | tf_op jit(solution)/shard_map/ppermute | solution.py:40
  42.1 28.4 %collective-permute-start.12 = (bf16[64,1024]{1,0:T(8,128)(2,1)S(1)}, bf16[64,1024]{1,0:T(8,128)(2,1)S(1)}, u32[]{:S(2)}, u32[]{:S(2)}) collective-permute-start(bf16[64,1024]{1,0:T(8,128)(2,1)S(1)} %get-tuple-element.42), channel_id=1, source_target_pairs={{0,64},{1,65},{2,66},{3,67},{4,68},{5,69},{6,70},{7,71},{8,72},{9,... | collective-permute-start | bytes 393224 | tf_op jit(solution)/shard_map/ppermute | solution.py:40
  42.7 33.8 %collective-permute-start.13 = (bf16[64,1024]{1,0:T(8,128)(2,1)S(1)}, bf16[64,1024]{1,0:T(8,128)(2,1)S(1)}, u32[]{:S(2)}, u32[]{:S(2)}) collective-permute-start(bf16[64,1024]{1,0:T(8,128)(2,1)S(1)} %get-tuple-element.43), channel_id=1, source_target_pairs={{0,128},{1,129},{2,130},{3,131},{4,132},{5,133},{6,134},{7,135},{8... | collective-permute-start | bytes 393224 | tf_op jit(solution)/shard_map/ppermute | solution.py:40
  70.5 6.1 %collective-permute-start.14 = (bf16[64,1024]{1,0:T(8,128)(2,1)S(1)}, bf16[64,1024]{1,0:T(8,128)(2,1)S(1)}, u32[]{:S(2)}, u32[]{:S(2)}) collective-permute-start(bf16[64,1024]{1,0:T(8,128)(2,1)S(1)} %get-tuple-element.44), channel_id=1, source_target_pairs={{0,192},{1,193},{2,194},{3,195},{4,196},{5,197},{6,198},{7,199},{8... | collective-permute-start | bytes 393224 | tf_op jit(solution)/shard_map/ppermute | solution.py:40
  82.2 10.2 %collective-permute-start.26 = (bf16[128,640]{1,0:T(8,128)(2,1)S(1)}, bf16[128,640]{1,0:T(8,128)(2,1)S(1)}, u32[]{:S(2)}, u32[]{:S(2)}) collective-permute-start(bf16[128,640]{1,0:T(8,128)(2,1)S(1)} %get-tuple-element.50), channel_id=1, source_target_pairs={{0,1},{1,2},{2,3},{3,0},{4,5},{5,6},{6,7},{7,4},{8,9},{9,10},{10,1... | collective-permute-start | bytes 491528 | tf_op jit(solution)/shard_map/ppermute | solution.py:40
  84.1 12.6 %collective-permute-start.27 = (bf16[128,640]{1,0:T(8,128)(2,1)S(1)}, bf16[128,640]{1,0:T(8,128)(2,1)S(1)}, u32[]{:S(2)}, u32[]{:S(2)}) collective-permute-start(bf16[128,640]{1,0:T(8,128)(2,1)S(1)} %get-tuple-element.51), channel_id=1, source_target_pairs={{0,33},{1,34},{2,35},{3,32},{4,37},{5,38},{6,39},{7,36},{8,41},{9,... | collective-permute-start | bytes 491528 | tf_op jit(solution)/shard_map/ppermute | solution.py:40
  87.2 16.0 %collective-permute-start.28 = (bf16[128,640]{1,0:T(8,128)(2,1)S(1)}, bf16[128,640]{1,0:T(8,128)(2,1)S(1)}, u32[]{:S(2)}, u32[]{:S(2)}) collective-permute-start(bf16[128,640]{1,0:T(8,128)(2,1)S(1)} %get-tuple-element.52), channel_id=1, source_target_pairs={{0,65},{1,66},{2,67},{3,64},{4,69},{5,70},{6,71},{7,68},{8,73},{9,... | collective-permute-start | bytes 491528 | tf_op jit(solution)/shard_map/ppermute | solution.py:40
  91.7 11.5 %collective-permute-start.29 = (bf16[128,640]{1,0:T(8,128)(2,1)S(1)}, bf16[128,640]{1,0:T(8,128)(2,1)S(1)}, u32[]{:S(2)}, u32[]{:S(2)}) collective-permute-start(bf16[128,640]{1,0:T(8,128)(2,1)S(1)} %get-tuple-element.53), channel_id=1, source_target_pairs={{0,97},{1,98},{2,99},{3,96},{4,101},{5,102},{6,103},{7,100},{8,105... | collective-permute-start | bytes 491528 | tf_op jit(solution)/shard_map/ppermute | solution.py:40
  91.7 14.3 %collective-permute-start.30 = (bf16[128,640]{1,0:T(8,128)(2,1)S(1)}, bf16[128,640]{1,0:T(8,128)(2,1)S(1)}, u32[]{:S(2)}, u32[]{:S(2)}) collective-permute-start(bf16[128,640]{1,0:T(8,128)(2,1)S(1)} %get-tuple-element.54), channel_id=1, source_target_pairs={{0,129},{1,130},{2,131},{3,128},{4,133},{5,134},{6,135},{7,132},{8... | collective-permute-start | bytes 491528 | tf_op jit(solution)/shard_map/ppermute | solution.py:40
  92.4 14.1 %collective-permute-start.31 = (bf16[128,640]{1,0:T(8,128)(2,1)S(1)}, bf16[128,640]{1,0:T(8,128)(2,1)S(1)}, u32[]{:S(2)}, u32[]{:S(2)}) collective-permute-start(bf16[128,640]{1,0:T(8,128)(2,1)S(1)} %get-tuple-element.55), channel_id=1, source_target_pairs={{0,161},{1,162},{2,163},{3,160},{4,165},{5,166},{6,167},{7,164},{8... | collective-permute-start | bytes 491528 | tf_op jit(solution)/shard_map/ppermute | solution.py:40
  96.7 13.5 %collective-permute-start.32 = (bf16[128,640]{1,0:T(8,128)(2,1)S(1)}, bf16[128,640]{1,0:T(8,128)(2,1)S(1)}, u32[]{:S(2)}, u32[]{:S(2)}) collective-permute-start(bf16[128,640]{1,0:T(8,128)(2,1)S(1)} %get-tuple-element.56), channel_id=1, source_target_pairs={{0,193},{1,194},{2,195},{3,192},{4,197},{5,198},{6,199},{7,196},{8... | collective-permute-start | bytes 491528 | tf_op jit(solution)/shard_map/ppermute | solution.py:40
  103.2 12.0 %collective-permute-start.33 = (bf16[128,640]{1,0:T(8,128)(2,1)S(1)}, bf16[128,640]{1,0:T(8,128)(2,1)S(1)}, u32[]{:S(2)}, u32[]{:S(2)}) collective-permute-start(bf16[128,640]{1,0:T(8,128)(2,1)S(1)} %get-tuple-element.57), channel_id=1, source_target_pairs={{0,225},{1,226},{2,227},{3,224},{4,229},{5,230},{6,231},{7,228},{8... | collective-permute-start | bytes 491528 | tf_op jit(solution)/shard_map/ppermute | solution.py:40
  103.2 13.2 %collective-permute-start.15 = (bf16[64,1024]{1,0:T(8,128)(2,1)S(1)}, bf16[64,1024]{1,0:T(8,128)(2,1)S(1)}, u32[]{:S(2)}, u32[]{:S(2)}) collective-permute-start(bf16[64,1024]{1,0:T(8,128)(2,1)S(1)} %shard_map.91.refs_8_.cross_ref), channel_id=1, source_target_pairs={{0,64},{1,65},{2,66},{3,67},{4,68},{5,69},{6,70},{7,71},{8,72},{9,... | collective-permute-start | bytes 393224 | tf_op jit(solution)/shard_map/ppermute | solution.py:40
  106.0 11.0 %collective-permute-start.16 = (bf16[64,1024]{1,0:T(8,128)(2,1)S(1)}, bf16[64,1024]{1,0:T(8,128)(2,1)S(1)}, u32[]{:S(2)}, u32[]{:S(2)}) collective-permute-start(bf16[64,1024]{1,0:T(8,128)(2,1)S(1)} %shard_map.91.refs_8_.cross_ref), channel_id=1, source_target_pairs={{0,128},{1,129},{2,130},{3,131},{4,132},{5,133},{6,134},{7,135},{8... | collective-permute-start | bytes 393224 | tf_op jit(solution)/shard_map/ppermute | solution.py:40
  106.5 10.5 %collective-permute-start.17 = (bf16[64,1024]{1,0:T(8,128)(2,1)S(1)}, bf16[64,1024]{1,0:T(8,128)(2,1)S(1)}, u32[]{:S(2)}, u32[]{:S(2)}) collective-permute-start(bf16[64,1024]{1,0:T(8,128)(2,1)S(1)} %shard_map.91.refs_8_.cross_ref), channel_id=1, source_target_pairs={{0,192},{1,193},{2,194},{3,195},{4,196},{5,197},{6,198},{7,199},{8... | collective-permute-start | bytes 393224 | tf_op jit(solution)/shard_map/ppermute | solution.py:40
  115.7 8.9 %collective-permute-start.34 = (bf16[128,640]{1,0:T(8,128)(2,1)S(1)}, bf16[128,640]{1,0:T(8,128)(2,1)S(1)}, u32[]{:S(2)}, u32[]{:S(2)}) collective-permute-start(bf16[128,640]{1,0:T(8,128)(2,1)S(1)} %get-tuple-element.59), channel_id=1, source_target_pairs={{0,4},{1,5},{2,6},{3,7},{4,8},{5,9},{6,10},{7,11},{8,12},{9,13},{1... | collective-permute-start | bytes 491528 | tf_op jit(solution)/shard_map/ppermute | solution.py:40
  116.4 8.3 %collective-permute-start.18 = (bf16[64,1024]{1,0:T(8,128)(2,1)S(1)}, bf16[64,1024]{1,0:T(8,128)(2,1)S(1)}, u32[]{:S(2)}, u32[]{:S(2)}) collective-permute-start(bf16[64,1024]{1,0:T(8,128)(2,1)S(1)} %shard_map.91.refs_8_.cross_ref), channel_id=1, source_target_pairs={{0,32},{1,33},{2,34},{3,35},{4,36},{5,37},{6,38},{7,39},{8,40},{9,... | collective-permute-start | bytes 393224 | tf_op jit(solution)/shard_map/ppermute | solution.py:40
  116.4 11.2 %collective-permute-start.19 = (bf16[64,1024]{1,0:T(8,128)(2,1)S(1)}, bf16[64,1024]{1,0:T(8,128)(2,1)S(1)}, u32[]{:S(2)}, u32[]{:S(2)}) collective-permute-start(bf16[64,1024]{1,0:T(8,128)(2,1)S(1)} %collective-permute-done.15.refs_9_), channel_id=1, source_target_pairs={{0,32},{1,33},{2,34},{3,35},{4,36},{5,37},{6,38},{7,39},{8,40},{9,... | collective-permute-start | bytes 393224 | tf_op jit(solution)/shard_map/ppermute | solution.py:40
  117.0 10.7 %collective-permute-start.20 = (bf16[64,1024]{1,0:T(8,128)(2,1)S(1)}, bf16[64,1024]{1,0:T(8,128)(2,1)S(1)}, u32[]{:S(2)}, u32[]{:S(2)}) collective-permute-start(bf16[64,1024]{1,0:T(8,128)(2,1)S(1)} %collective-permute-done.16.refs_10_), channel_id=1, source_target_pairs={{0,32},{1,33},{2,34},{3,35},{4,36},{5,37},{6,38},{7,39},{8,40},{9,... | collective-permute-start | bytes 393224 | tf_op jit(solution)/shard_map/ppermute | solution.py:40
  117.1 10.6 %collective-permute-start.21 = (bf16[64,1024]{1,0:T(8,128)(2,1)S(1)}, bf16[64,1024]{1,0:T(8,128)(2,1)S(1)}, u32[]{:S(2)}, u32[]{:S(2)}) collective-permute-start(bf16[64,1024]{1,0:T(8,128)(2,1)S(1)} %collective-permute-done.17.refs_11_), channel_id=1, source_target_pairs={{0,32},{1,33},{2,34},{3,35},{4,36},{5,37},{6,38},{7,39},{8,40},{9,... | collective-permute-start | bytes 393224 | tf_op jit(solution)/shard_map/ppermute | solution.py:40
  124.7 7.0 %collective-permute-start.35 = (f32[128,128]{1,0:T(8,128)S(1)}, f32[128,128]{1,0:T(8,128)S(1)}, u32[]{:S(2)}, u32[]{:S(2)}) collective-permute-start(f32[128,128]{1,0:T(8,128)S(1)} %get-tuple-element.61), channel_id=1, source_target_pairs={{0,224},{1,225},{2,226},{3,227},{4,228},{5,229},{6,230},{7,231},{8... | collective-permute-start | bytes 196616 | tf_op jit(solution)/shard_map/ppermute | solution.py:40
  124.7 7.0 %collective-permute-start.36 = (f32[128,128]{1,0:T(8,128)S(1)}, f32[128,128]{1,0:T(8,128)S(1)}, u32[]{:S(2)}, u32[]{:S(2)}) collective-permute-start(f32[128,128]{1,0:T(8,128)S(1)} %get-tuple-element.62), channel_id=1, source_target_pairs={{0,192},{1,193},{2,194},{3,195},{4,196},{5,197},{6,198},{7,199},{8... | collective-permute-start | bytes 196616 | tf_op jit(solution)/shard_map/ppermute | solution.py:40
  (13 other events, 152.7 us)

commit v2 on v1

--- a/solution.py
+++ b/solution.py
@@ -408,7 +408,9 @@
     others = shifted(others, along_x)
     cross = cross_total(inverse, own, others)
     blocks = tile_call(own_sum, cross, dinv, rows)
-    arrived = shifted(blocks, lambda i: to_column(i // 2, i % 2), 0)
+    arrived = [None] * NU
+    for i in ORDER:
+        arrived[i] = perm(blocks[i], to_column(i // 2, i % 2))
     crosses = gathered(cross)
     here, onward = arrived_sum(arrived)
     onward = [perm(onward, along_z(1))]
@@ -417,6 +419,9 @@
     panel_out = rows_call(panel, dinv, sums, crosses)
     diag_out = diag_call(diag_tiles[0], total, mirrored)
     return (panel_out[None], diag_out[None])
+
+
+ORDER = (2, 6, 3, 7, 4, 5, 0, 1)
 
 
 def solution(mesh):

time: 134 us -> 134 us (level)
  no operation moved by 1% of the time
where the time goes in v2:
time: 134 us
  starting transfers between devices  55 us (41%)
  waiting for transfers between devices  50.9 us (38%)
  Pallas kernels  26.1 us (19%)
    ppermute x38, starting transfers between devices, perm(): return lax.ppermute(block, AXES, pairs)  55 us
    ppermute x38, waiting for transfers between devices, perm(): return lax.ppermute(block, AXES, pairs)  50.9 us
    pallas_call x12, Pallas kernels, call(): pl.pallas_call(kernel, out_shape=shapes, in_specs=[pl.BlockSpec(memory_sp...  19.8 us
    pallas_call x1, Pallas kernels, sketch_call(): pl.pallas_call(sketch_kernel, out_shape=[pltpu.VMEM(out, BF16), pltpu.VME...  5.43 us
  transfers between devices with their start and end apart: 38, of which 12 were waited for; matrix products, arithmetic and copies ran while one was open for 0% of the time, Pallas kernels for 11%

profile of v2, /device:TPU:1, one launch (start us, length us, event | category | flops | bytes accessed | tf_op | source)
XLA Modules:
  0.0 133.8 jit_solution(9100463816612025256)
XLA Ops:
  1.4 5.4 %sketch_product.1 = (bf16[4,64,1024]{2,1,0:T(8,128)(2,1)S(1)}, f32[4,64,1024]{2,1,0:T(8,128)S(1)}) custom-call(s32[8]{0:T(128)S(1)} %bitcast.18, bf16[8,96,1024]{2,1,0:T(8,128)(2,1)} %bitcast.13, bf16[8,96,1024]{2,1,0:T(8,128)(2,1)} %bitcast.15, bf16[64,1024]{1,0:T(8,128)(2,1)} %bitcast.22), custom_call_target="tpu_custom_call" | custom-call | tf_op jit(solution)/shard_map/sketch_product/pallas_call | solution.py:121
  6.9 3.3 %collective-permute-start = (bf16[4,64,1024]{2,1,0:T(8,128)(2,1)S(1)}, bf16[4,64,1024]{2,1,0:T(8,128)(2,1)S(1)}, u32[]{:S(2)}, u32[]{:S(2)}) collective-permute-start(bf16[4,64,1024]{2,1,0:T(8,128)(2,1)S(1)} %get-tuple-element.34), channel_id=1, source_target_pairs={{0,32},{1,33},{2,34},{3,35},{4,36},{5,37},{6,38},{7,39},{8,40},{9,... | collective-permute-start | bytes 1572872 | tf_op jit(solution)/shard_map/ppermute | solution.py:40
  10.5 1.2 collective-permute-done.got_ref
  11.9 1.9 %collective-permute-start.2 = (bf16[64,1024]{1,0:T(8,128)(2,1)S(1)}, bf16[64,1024]{1,0:T(8,128)(2,1)S(1)}, u32[]{:S(2)}, u32[]{:S(2)}) collective-permute-start(bf16[64,1024]{1,0:T(8,128)(2,1)S(1)} %get-tuple-element.37), channel_id=1, source_target_pairs={{0,128},{1,129},{2,130},{3,131},{4,132},{5,133},{6,134},{7,135},{8... | collective-permute-start | bytes 393224 | tf_op jit(solution)/shard_map/ppermute | solution.py:40
  13.8 1.2 collective-permute-start.3
  15.0 3.5 %collective-permute-done.1.a_ref = bf16[64,1024]{1,0:T(8,128)(2,1)S(1)} collective-permute-done((bf16[64,1024]{1,0:T(8,128)(2,1)S(1)}, bf16[64,1024]{1,0:T(8,128)(2,1)S(1)}, u32[]{:S(2)}, u32[]{:S(2)}) %collective-permute-start.1) | collective-permute-done | bytes 131104 | tf_op jit(solution)/shard_map/ppermute | solution.py:40
  18.5 1.4 %collective-permute-done.2.b_ref = bf16[64,1024]{1,0:T(8,128)(2,1)S(1)} collective-permute-done((bf16[64,1024]{1,0:T(8,128)(2,1)S(1)}, bf16[64,1024]{1,0:T(8,128)(2,1)S(1)}, u32[]{:S(2)}, u32[]{:S(2)}) %collective-permute-start.2) | collective-permute-done | bytes 131104 | tf_op jit(solution)/shard_map/ppermute | solution.py:40
  21.0 3.5 %collective-permute-start.6 = (bf16[64,1024]{1,0:T(8,128)(2,1)S(1)}, bf16[64,1024]{1,0:T(8,128)(2,1)S(1)}, u32[]{:S(2)}, u32[]{:S(2)}) collective-permute-start(bf16[64,1024]{1,0:T(8,128)(2,1)S(1)} %shard_map.87.summed_ref.refs_0_.basis_ref), channel_id=1, source_target_pairs={{0,192},{1,193},{2,194},{3,195},{4,196},{5,197},{6,198},{7,199},{8... | collective-permute-start | bytes 393224 | tf_op jit(solution)/shard_map/ppermute | solution.py:40
  24.4 1.3 collective-permute-start.5
  26.8 1.3 %collective-permute-start.10 = (bf16[64,1024]{1,0:T(8,128)(2,1)S(1)}, bf16[64,1024]{1,0:T(8,128)(2,1)S(1)}, u32[]{:S(2)}, u32[]{:S(2)}) collective-permute-start(bf16[64,1024]{1,0:T(8,128)(2,1)S(1)} %collective-permute-done.6.refs_3_), channel_id=1, source_target_pairs={{0,32},{1,33},{2,34},{3,35},{4,36},{5,37},{6,38},{7,39},{8,40},{9,... | collective-permute-start | bytes 393224 | tf_op jit(solution)/shard_map/ppermute | solution.py:40
  28.1 5.0 %collective-permute-done.4.refs_1_ = bf16[64,1024]{1,0:T(8,128)(2,1)S(1)} collective-permute-done((bf16[64,1024]{1,0:T(8,128)(2,1)S(1)}, bf16[64,1024]{1,0:T(8,128)(2,1)S(1)}, u32[]{:S(2)}, u32[]{:S(2)}) %collective-permute-start.4) | collective-permute-done | bytes 131104 | tf_op jit(solution)/shard_map/ppermute | solution.py:40
  33.1 1.2 collective-permute-start.8
  35.7 3.1 %shard_map.89 = (bf16[4,64,1024]{2,1,0:T(8,128)(2,1)S(1)}, f32[4,64,1024]{2,1,0:T(8,128)S(1)}) custom-call(s32[8]{0:T(128)S(1)} %bitcast.19, bf16[8,96,1024]{2,1,0:T(8,128)(2,1)S(1)} %bitcast.16, bf16[8,96,1024]{2,1,0:T(8,128)(2,1)S(1)} %bitcast.14, bf16[64,1024]{1,0:T(8,128)(2,1)S(1)} %shard_map.87.summed_ref.refs_0_.basis_ref, ...), custom_call_target="tpu_custom_call" | custom-call | tf_op jit(solution)/shard_map/pallas_call | solution.py:75
  39.3 1.3 collective-permute-start.24
  40.5 1.4 %collective-permute-start.25 = (bf16[2,128,1024]{2,1,0:T(8,128)(2,1)S(1)}, bf16[2,128,1024]{2,1,0:T(8,128)(2,1)S(1)}, u32[]{:S(2)}, u32[]{:S(2)}) collective-permute-start(bf16[2,128,1024]{2,1,0:T(8,128)(2,1)S(1)} %get-tuple-element.49), channel_id=1, source_target_pairs={{0,192},{1,193},{2,194},{3,195},{4,196},{5,197},{6,198},{7,199},{8... | collective-permute-start | bytes 1572872 | tf_op jit(solution)/shard_map/ppermute | solution.py:40
  42.7 1.9 %collective-permute-start.13 = (bf16[64,1024]{1,0:T(8,128)(2,1)S(1)}, bf16[64,1024]{1,0:T(8,128)(2,1)S(1)}, u32[]{:S(2)}, u32[]{:S(2)}) collective-permute-start(bf16[64,1024]{1,0:T(8,128)(2,1)S(1)} %get-tuple-element.43), channel_id=1, source_target_pairs={{0,128},{1,129},{2,130},{3,131},{4,132},{5,133},{6,134},{7,135},{8... | collective-permute-start | bytes 393224 | tf_op jit(solution)/shard_map/ppermute | solution.py:40
  44.6 25.9 %collective-permute-done.12.a_ref = bf16[64,1024]{1,0:T(8,128)(2,1)S(1)} collective-permute-done((bf16[64,1024]{1,0:T(8,128)(2,1)S(1)}, bf16[64,1024]{1,0:T(8,128)(2,1)S(1)}, u32[]{:S(2)}, u32[]{:S(2)}) %collective-permute-start.12) | collective-permute-done | bytes 131104 | tf_op jit(solution)/shard_map/ppermute | solution.py:40
  70.5 6.1 %shard_map.88.inverse_ref = f32[64,64]{1,0:T(8,128)S(1)} custom-call(bf16[64,1024]{1,0:T(8,128)(2,1)S(1)} %shard_map.87.summed_ref.refs_0_.basis_ref), custom_call_target="tpu_custom_call" | custom-call | tf_op jit(solution)/shard_map/pallas_call | solution.py:75
  77.0 5.2 %shard_map.95 = (bf16[128,640]{1,0:T(8,128)(2,1)S(1)}, bf16[128,640]{1,0:T(8,128)(2,1)S(1)}, bf16[128,640]{1,0:T(8,128)(2,1)S(1)}, bf16[128,640]{1,0:T(8,128)(2,...) custom-call(bf16[64,1024]{1,0:T(8,128)(2,1)S(1)} %shard_map.87.summe, ...), custom_call_target="tpu_custom_call" | custom-call | tf_op jit(solution)/shard_map/pallas_call | solution.py:75
  82.2 1.9 %collective-permute-start.26 = (bf16[128,640]{1,0:T(8,128)(2,1)S(1)}, bf16[128,640]{1,0:T(8,128)(2,1)S(1)}, u32[]{:S(2)}, u32[]{:S(2)}) collective-permute-start(bf16[128,640]{1,0:T(8,128)(2,1)S(1)} %get-tuple-element.50), channel_id=1, source_target_pairs={{0,1},{1,2},{2,3},{3,0},{4,5},{5,6},{6,7},{7,4},{8,9},{9,10},{10,1... | collective-permute-start | bytes 491528 | tf_op jit(solution)/shard_map/ppermute | solution.py:40
  84.1 3.1 %collective-permute-start.27 = (bf16[128,640]{1,0:T(8,128)(2,1)S(1)}, bf16[128,640]{1,0:T(8,128)(2,1)S(1)}, u32[]{:S(2)}, u32[]{:S(2)}) collective-permute-start(bf16[128,640]{1,0:T(8,128)(2,1)S(1)} %get-tuple-element.51), channel_id=1, source_target_pairs={{0,33},{1,34},{2,35},{3,32},{4,37},{5,38},{6,39},{7,36},{8,41},{9,... | collective-permute-start | bytes 491528 | tf_op jit(solution)/shard_map/ppermute | solution.py:40
  87.2 4.5 %collective-permute-start.28 = (bf16[128,640]{1,0:T(8,128)(2,1)S(1)}, bf16[128,640]{1,0:T(8,128)(2,1)S(1)}, u32[]{:S(2)}, u32[]{:S(2)}) collective-permute-start(bf16[128,640]{1,0:T(8,128)(2,1)S(1)} %get-tuple-element.52), channel_id=1, source_target_pairs={{0,65},{1,66},{2,67},{3,64},{4,69},{5,70},{6,71},{7,68},{8,73},{9,... | collective-permute-start | bytes 491528 | tf_op jit(solution)/shard_map/ppermute | solution.py:40
  92.4 3.7 %collective-permute-start.31 = (bf16[128,640]{1,0:T(8,128)(2,1)S(1)}, bf16[128,640]{1,0:T(8,128)(2,1)S(1)}, u32[]{:S(2)}, u32[]{:S(2)}) collective-permute-start(bf16[128,640]{1,0:T(8,128)(2,1)S(1)} %get-tuple-element.55), channel_id=1, source_target_pairs={{0,161},{1,162},{2,163},{3,160},{4,165},{5,166},{6,167},{7,164},{8... | collective-permute-start | bytes 491528 | tf_op jit(solution)/shard_map/ppermute | solution.py:40
  96.7 6.5 %collective-permute-start.32 = (bf16[128,640]{1,0:T(8,128)(2,1)S(1)}, bf16[128,640]{1,0:T(8,128)(2,1)S(1)}, u32[]{:S(2)}, u32[]{:S(2)}) collective-permute-start(bf16[128,640]{1,0:T(8,128)(2,1)S(1)} %get-tuple-element.56), channel_id=1, source_target_pairs={{0,193},{1,194},{2,195},{3,192},{4,197},{5,198},{6,199},{7,196},{8... | collective-permute-start | bytes 491528 | tf_op jit(solution)/shard_map/ppermute | solution.py:40
  103.2 2.8 %collective-permute-start.15 = (bf16[64,1024]{1,0:T(8,128)(2,1)S(1)}, bf16[64,1024]{1,0:T(8,128)(2,1)S(1)}, u32[]{:S(2)}, u32[]{:S(2)}) collective-permute-start(bf16[64,1024]{1,0:T(8,128)(2,1)S(1)} %shard_map.91.refs_8_.cross_ref), channel_id=1, source_target_pairs={{0,64},{1,65},{2,66},{3,67},{4,68},{5,69},{6,70},{7,71},{8,72},{9,... | collective-permute-start | bytes 393224 | tf_op jit(solution)/shard_map/ppermute | solution.py:40
  106.5 3.6 %collective-permute-start.17 = (bf16[64,1024]{1,0:T(8,128)(2,1)S(1)}, bf16[64,1024]{1,0:T(8,128)(2,1)S(1)}, u32[]{:S(2)}, u32[]{:S(2)}) collective-permute-start(bf16[64,1024]{1,0:T(8,128)(2,1)S(1)} %shard_map.91.refs_8_.cross_ref), channel_id=1, source_target_pairs={{0,192},{1,193},{2,194},{3,195},{4,196},{5,197},{6,198},{7,199},{8... | collective-permute-start | bytes 393224 | tf_op jit(solution)/shard_map/ppermute | solution.py:40
  110.2 5.1 %collective-permute-done.33.refs_7_ = bf16[128,640]{1,0:T(8,128)(2,1)S(1)} collective-permute-done((bf16[128,640]{1,0:T(8,128)(2,1)S(1)}, bf16[128,640]{1,0:T(8,128)(2,1)S(1)}, u32[]{:S(2)}, u32[]{:S(2)}) %collective-permute-start.33) | collective-permute-done | bytes 163872 | tf_op jit(solution)/shard_map/ppermute | solution.py:40
  117.1 2.7 %collective-permute-start.21 = (bf16[64,1024]{1,0:T(8,128)(2,1)S(1)}, bf16[64,1024]{1,0:T(8,128)(2,1)S(1)}, u32[]{:S(2)}, u32[]{:S(2)}) collective-permute-start(bf16[64,1024]{1,0:T(8,128)(2,1)S(1)} %collective-permute-done.17.refs_11_), channel_id=1, source_target_pairs={{0,32},{1,33},{2,34},{3,35},{4,36},{5,37},{6,38},{7,39},{8,40},{9,... | collective-permute-start | bytes 393224 | tf_op jit(solution)/shard_map/ppermute | solution.py:40
  119.8 4.8 %collective-permute-done.34.onward_ref = bf16[128,640]{1,0:T(8,128)(2,1)S(1)} collective-permute-done((bf16[128,640]{1,0:T(8,128)(2,1)S(1)}, bf16[128,640]{1,0:T(8,128)(2,1)S(1)}, u32[]{:S(2)}, u32[]{:S(2)}) %collective-permute-start.34) | collective-permute-done | bytes 163872 | tf_op jit(solution)/shard_map/ppermute | solution.py:40
  124.7 2.9 %collective-permute-start.36 = (f32[128,128]{1,0:T(8,128)S(1)}, f32[128,128]{1,0:T(8,128)S(1)}, u32[]{:S(2)}, u32[]{:S(2)}) collective-permute-start(f32[128,128]{1,0:T(8,128)S(1)} %get-tuple-element.62), channel_id=1, source_target_pairs={{0,192},{1,193},{2,194},{3,195},{4,196},{5,197},{6,198},{7,199},{8... | collective-permute-start | bytes 196616 | tf_op jit(solution)/shard_map/ppermute | solution.py:40
  127.7 4.0 %shard_map.92 = bf16[8,128,1024]{2,1,0:T(8,128)(2,1)} custom-call(bf16[8,128,1024]{2,1,0:T(8,128)(2,1)S(1)} %bitcast.12, bf16[1024,1024]{1,0:T(8,128)(2,1)S(1)} %bitcast.10, bf16[64,1024]{1,0:T(8,128)(2,1)S(1)} %shard_map.87.summed_ref.refs_0_.basis_ref, bf16[64,1024]{1,0:T(8,128)(2,1)S(1)} %collective-permute-done.4.refs_1_, ...), custom_call_target="tpu_custom_call" | custom-call | tf_op jit(solution)/shard_map/pallas_call | solution.py:75
  131.7 1.1 collective-permute-done.37.c_ref
  (72 shorter events, 11.0 us)
Async XLA Ops:
  10.3 28.7 %collective-permute-start.22 = (bf16[4,128,1024]{2,1,0:T(8,128)(2,1)S(1)}, bf16[4,128,1024]{2,1,0:T(8,128)(2,1)S(1)}, u32[]{:S(2)}, u32[]{:S(2)}) collective-permute-start(bf16[4,128,1024]{2,1,0:T(8,128)(2,1)S(1)} %get-tuple-element.46), channel_id=1, source_target_pairs={{0,32},{1,33},{2,34},{3,35},{4,36},{5,37},{6,38},{7,39},{8,40},{9,... | collective-permute-start | bytes 3145736 | tf_op jit(solution)/shard_map/ppermute | solution.py:40
  11.8 6.7 %collective-permute-start.1 = (bf16[64,1024]{1,0:T(8,128)(2,1)S(1)}, bf16[64,1024]{1,0:T(8,128)(2,1)S(1)}, u32[]{:S(2)}, u32[]{:S(2)}) collective-permute-start(bf16[64,1024]{1,0:T(8,128)(2,1)S(1)} %get-tuple-element.36), channel_id=1, source_target_pairs={{0,64},{1,65},{2,66},{3,67},{4,68},{5,69},{6,70},{7,71},{8,72},{9,... | collective-permute-start | bytes 393224 | tf_op jit(solution)/shard_map/ppermute | solution.py:40
  11.9 8.0 %collective-permute-start.2 = (bf16[64,1024]{1,0:T(8,128)(2,1)S(1)}, bf16[64,1024]{1,0:T(8,128)(2,1)S(1)}, u32[]{:S(2)}, u32[]{:S(2)}) collective-permute-start(bf16[64,1024]{1,0:T(8,128)(2,1)S(1)} %get-tuple-element.37), channel_id=1, source_target_pairs={{0,128},{1,129},{2,130},{3,131},{4,132},{5,133},{6,134},{7,135},{8... | collective-permute-start | bytes 393224 | tf_op jit(solution)/shard_map/ppermute | solution.py:40
  13.8 7.0 %collective-permute-start.3 = (bf16[64,1024]{1,0:T(8,128)(2,1)S(1)}, bf16[64,1024]{1,0:T(8,128)(2,1)S(1)}, u32[]{:S(2)}, u32[]{:S(2)}) collective-permute-start(bf16[64,1024]{1,0:T(8,128)(2,1)S(1)} %get-tuple-element.38), channel_id=1, source_target_pairs={{0,192},{1,193},{2,194},{3,195},{4,196},{5,197},{6,198},{7,199},{8... | collective-permute-start | bytes 393224 | tf_op jit(solution)/shard_map/ppermute | solution.py:40
  24.4 8.7 %collective-permute-start.4 = (bf16[64,1024]{1,0:T(8,128)(2,1)S(1)}, bf16[64,1024]{1,0:T(8,128)(2,1)S(1)}, u32[]{:S(2)}, u32[]{:S(2)}) collective-permute-start(bf16[64,1024]{1,0:T(8,128)(2,1)S(1)} %shard_map.87.summed_ref.refs_0_.basis_ref), channel_id=1, source_target_pairs={{0,64},{1,65},{2,66},{3,67},{4,68},{5,69},{6,70},{7,71},{8,72},{9,... | collective-permute-start | bytes 393224 | tf_op jit(solution)/shard_map/ppermute | solution.py:40
  24.4 9.9 %collective-permute-start.5 = (bf16[64,1024]{1,0:T(8,128)(2,1)S(1)}, bf16[64,1024]{1,0:T(8,128)(2,1)S(1)}, u32[]{:S(2)}, u32[]{:S(2)}) collective-permute-start(bf16[64,1024]{1,0:T(8,128)(2,1)S(1)} %shard_map.87.summed_ref.refs_0_.basis_ref), channel_id=1, source_target_pairs={{0,128},{1,129},{2,130},{3,131},{4,132},{5,133},{6,134},{7,135},{8... | collective-permute-start | bytes 393224 | tf_op jit(solution)/shard_map/ppermute | solution.py:40
  25.7 8.7 %collective-permute-start.7 = (bf16[64,1024]{1,0:T(8,128)(2,1)S(1)}, bf16[64,1024]{1,0:T(8,128)(2,1)S(1)}, u32[]{:S(2)}, u32[]{:S(2)}) collective-permute-start(bf16[64,1024]{1,0:T(8,128)(2,1)S(1)} %shard_map.87.summed_ref.refs_0_.basis_ref), channel_id=1, source_target_pairs={{0,32},{1,33},{2,34},{3,35},{4,36},{5,37},{6,38},{7,39},{8,40},{9,... | collective-permute-start | bytes 393224 | tf_op jit(solution)/shard_map/ppermute | solution.py:40
  26.8 7.6 %collective-permute-start.10 = (bf16[64,1024]{1,0:T(8,128)(2,1)S(1)}, bf16[64,1024]{1,0:T(8,128)(2,1)S(1)}, u32[]{:S(2)}, u32[]{:S(2)}) collective-permute-start(bf16[64,1024]{1,0:T(8,128)(2,1)S(1)} %collective-permute-done.6.refs_3_), channel_id=1, source_target_pairs={{0,32},{1,33},{2,34},{3,35},{4,36},{5,37},{6,38},{7,39},{8,40},{9,... | collective-permute-start | bytes 393224 | tf_op jit(solution)/shard_map/ppermute | solution.py:40
  39.2 37.8 %collective-permute-start.23 = (bf16[2,128,1024]{2,1,0:T(8,128)(2,1)S(1)}, bf16[2,128,1024]{2,1,0:T(8,128)(2,1)S(1)}, u32[]{:S(2)}, u32[]{:S(2)}) collective-permute-start(bf16[2,128,1024]{2,1,0:T(8,128)(2,1)S(1)} %get-tuple-element.47), channel_id=1, source_target_pairs={{0,64},{1,65},{2,66},{3,67},{4,68},{5,69},{6,70},{7,71},{8,72},{9,... | collective-permute-start | bytes 1572872 | tf_op jit(solution)/shard_map/ppermute | solution.py:40
  39.3 37.7 %collective-permute-start.24 = (bf16[2,128,1024]{2,1,0:T(8,128)(2,1)S(1)}, bf16[2,128,1024]{2,1,0:T(8,128)(2,1)S(1)}, u32[]{:S(2)}, u32[]{:S(2)}) collective-permute-start(bf16[2,128,1024]{2,1,0:T(8,128)(2,1)S(1)} %get-tuple-element.48), channel_id=1, source_target_pairs={{0,128},{1,129},{2,130},{3,131},{4,132},{5,133},{6,134},{7,135},{8... | collective-permute-start | bytes 1572872 | tf_op jit(solution)/shard_map/ppermute | solution.py:40
  40.5 36.5 %collective-permute-start.25 = (bf16[2,128,1024]{2,1,0:T(8,128)(2,1)S(1)}, bf16[2,128,1024]{2,1,0:T(8,128)(2,1)S(1)}, u32[]{:S(2)}, u32[]{:S(2)}) collective-permute-start(bf16[2,128,1024]{2,1,0:T(8,128)(2,1)S(1)} %get-tuple-element.49), channel_id=1, source_target_pairs={{0,192},{1,193},{2,194},{3,195},{4,196},{5,197},{6,198},{7,199},{8... | collective-permute-start | bytes 1572872 | tf_op jit(solution)/shard_map/ppermute | solution.py:40
  42.1 28.4 %collective-permute-start.12 = (bf16[64,1024]{1,0:T(8,128)(2,1)S(1)}, bf16[64,1024]{1,0:T(8,128)(2,1)S(1)}, u32[]{:S(2)}, u32[]{:S(2)}) collective-permute-start(bf16[64,1024]{1,0:T(8,128)(2,1)S(1)} %get-tuple-element.42), channel_id=1, source_target_pairs={{0,64},{1,65},{2,66},{3,67},{4,68},{5,69},{6,70},{7,71},{8,72},{9,... | collective-permute-start | bytes 393224 | tf_op jit(solution)/shard_map/ppermute | solution.py:40
  42.7 33.8 %collective-permute-start.13 = (bf16[64,1024]{1,0:T(8,128)(2,1)S(1)}, bf16[64,1024]{1,0:T(8,128)(2,1)S(1)}, u32[]{:S(2)}, u32[]{:S(2)}) collective-permute-start(bf16[64,1024]{1,0:T(8,128)(2,1)S(1)} %get-tuple-element.43), channel_id=1, source_target_pairs={{0,128},{1,129},{2,130},{3,131},{4,132},{5,133},{6,134},{7,135},{8... | collective-permute-start | bytes 393224 | tf_op jit(solution)/shard_map/ppermute | solution.py:40
  70.5 6.1 %collective-permute-start.14 = (bf16[64,1024]{1,0:T(8,128)(2,1)S(1)}, bf16[64,1024]{1,0:T(8,128)(2,1)S(1)}, u32[]{:S(2)}, u32[]{:S(2)}) collective-permute-start(bf16[64,1024]{1,0:T(8,128)(2,1)S(1)} %get-tuple-element.44), channel_id=1, source_target_pairs={{0,192},{1,193},{2,194},{3,195},{4,196},{5,197},{6,198},{7,199},{8... | collective-permute-start | bytes 393224 | tf_op jit(solution)/shard_map/ppermute | solution.py:40
  82.2 10.2 %collective-permute-start.26 = (bf16[128,640]{1,0:T(8,128)(2,1)S(1)}, bf16[128,640]{1,0:T(8,128)(2,1)S(1)}, u32[]{:S(2)}, u32[]{:S(2)}) collective-permute-start(bf16[128,640]{1,0:T(8,128)(2,1)S(1)} %get-tuple-element.50), channel_id=1, source_target_pairs={{0,1},{1,2},{2,3},{3,0},{4,5},{5,6},{6,7},{7,4},{8,9},{9,10},{10,1... | collective-permute-start | bytes 491528 | tf_op jit(solution)/shard_map/ppermute | solution.py:40
  84.1 12.6 %collective-permute-start.27 = (bf16[128,640]{1,0:T(8,128)(2,1)S(1)}, bf16[128,640]{1,0:T(8,128)(2,1)S(1)}, u32[]{:S(2)}, u32[]{:S(2)}) collective-permute-start(bf16[128,640]{1,0:T(8,128)(2,1)S(1)} %get-tuple-element.51), channel_id=1, source_target_pairs={{0,33},{1,34},{2,35},{3,32},{4,37},{5,38},{6,39},{7,36},{8,41},{9,... | collective-permute-start | bytes 491528 | tf_op jit(solution)/shard_map/ppermute | solution.py:40
  87.2 16.0 %collective-permute-start.28 = (bf16[128,640]{1,0:T(8,128)(2,1)S(1)}, bf16[128,640]{1,0:T(8,128)(2,1)S(1)}, u32[]{:S(2)}, u32[]{:S(2)}) collective-permute-start(bf16[128,640]{1,0:T(8,128)(2,1)S(1)} %get-tuple-element.52), channel_id=1, source_target_pairs={{0,65},{1,66},{2,67},{3,64},{4,69},{5,70},{6,71},{7,68},{8,73},{9,... | collective-permute-start | bytes 491528 | tf_op jit(solution)/shard_map/ppermute | solution.py:40
  91.7 11.5 %collective-permute-start.29 = (bf16[128,640]{1,0:T(8,128)(2,1)S(1)}, bf16[128,640]{1,0:T(8,128)(2,1)S(1)}, u32[]{:S(2)}, u32[]{:S(2)}) collective-permute-start(bf16[128,640]{1,0:T(8,128)(2,1)S(1)} %get-tuple-element.53), channel_id=1, source_target_pairs={{0,97},{1,98},{2,99},{3,96},{4,101},{5,102},{6,103},{7,100},{8,105... | collective-permute-start | bytes 491528 | tf_op jit(solution)/shard_map/ppermute | solution.py:40
  91.7 14.3 %collective-permute-start.30 = (bf16[128,640]{1,0:T(8,128)(2,1)S(1)}, bf16[128,640]{1,0:T(8,128)(2,1)S(1)}, u32[]{:S(2)}, u32[]{:S(2)}) collective-permute-start(bf16[128,640]{1,0:T(8,128)(2,1)S(1)} %get-tuple-element.54), channel_id=1, source_target_pairs={{0,129},{1,130},{2,131},{3,128},{4,133},{5,134},{6,135},{7,132},{8... | collective-permute-start | bytes 491528 | tf_op jit(solution)/shard_map/ppermute | solution.py:40
  92.4 14.1 %collective-permute-start.31 = (bf16[128,640]{1,0:T(8,128)(2,1)S(1)}, bf16[128,640]{1,0:T(8,128)(2,1)S(1)}, u32[]{:S(2)}, u32[]{:S(2)}) collective-permute-start(bf16[128,640]{1,0:T(8,128)(2,1)S(1)} %get-tuple-element.55), channel_id=1, source_target_pairs={{0,161},{1,162},{2,163},{3,160},{4,165},{5,166},{6,167},{7,164},{8... | collective-permute-start | bytes 491528 | tf_op jit(solution)/shard_map/ppermute | solution.py:40
  96.7 13.5 %collective-permute-start.32 = (bf16[128,640]{1,0:T(8,128)(2,1)S(1)}, bf16[128,640]{1,0:T(8,128)(2,1)S(1)}, u32[]{:S(2)}, u32[]{:S(2)}) collective-permute-start(bf16[128,640]{1,0:T(8,128)(2,1)S(1)} %get-tuple-element.56), channel_id=1, source_target_pairs={{0,193},{1,194},{2,195},{3,192},{4,197},{5,198},{6,199},{7,196},{8... | collective-permute-start | bytes 491528 | tf_op jit(solution)/shard_map/ppermute | solution.py:40
  103.2 12.0 %collective-permute-start.33 = (bf16[128,640]{1,0:T(8,128)(2,1)S(1)}, bf16[128,640]{1,0:T(8,128)(2,1)S(1)}, u32[]{:S(2)}, u32[]{:S(2)}) collective-permute-start(bf16[128,640]{1,0:T(8,128)(2,1)S(1)} %get-tuple-element.57), channel_id=1, source_target_pairs={{0,225},{1,226},{2,227},{3,224},{4,229},{5,230},{6,231},{7,228},{8... | collective-permute-start | bytes 491528 | tf_op jit(solution)/shard_map/ppermute | solution.py:40
  103.2 13.2 %collective-permute-start.15 = (bf16[64,1024]{1,0:T(8,128)(2,1)S(1)}, bf16[64,1024]{1,0:T(8,128)(2,1)S(1)}, u32[]{:S(2)}, u32[]{:S(2)}) collective-permute-start(bf16[64,1024]{1,0:T(8,128)(2,1)S(1)} %shard_map.91.refs_8_.cross_ref), channel_id=1, source_target_pairs={{0,64},{1,65},{2,66},{3,67},{4,68},{5,69},{6,70},{7,71},{8,72},{9,... | collective-permute-start | bytes 393224 | tf_op jit(solution)/shard_map/ppermute | solution.py:40
  106.0 11.0 %collective-permute-start.16 = (bf16[64,1024]{1,0:T(8,128)(2,1)S(1)}, bf16[64,1024]{1,0:T(8,128)(2,1)S(1)}, u32[]{:S(2)}, u32[]{:S(2)}) collective-permute-start(bf16[64,1024]{1,0:T(8,128)(2,1)S(1)} %shard_map.91.refs_8_.cross_ref), channel_id=1, source_target_pairs={{0,128},{1,129},{2,130},{3,131},{4,132},{5,133},{6,134},{7,135},{8... | collective-permute-start | bytes 393224 | tf_op jit(solution)/shard_map/ppermute | solution.py:40
  106.5 10.5 %collective-permute-start.17 = (bf16[64,1024]{1,0:T(8,128)(2,1)S(1)}, bf16[64,1024]{1,0:T(8,128)(2,1)S(1)}, u32[]{:S(2)}, u32[]{:S(2)}) collective-permute-start(bf16[64,1024]{1,0:T(8,128)(2,1)S(1)} %shard_map.91.refs_8_.cross_ref), channel_id=1, source_target_pairs={{0,192},{1,193},{2,194},{3,195},{4,196},{5,197},{6,198},{7,199},{8... | collective-permute-start | bytes 393224 | tf_op jit(solution)/shard_map/ppermute | solution.py:40
  115.7 8.9 %collective-permute-start.34 = (bf16[128,640]{1,0:T(8,128)(2,1)S(1)}, bf16[128,640]{1,0:T(8,128)(2,1)S(1)}, u32[]{:S(2)}, u32[]{:S(2)}) collective-permute-start(bf16[128,640]{1,0:T(8,128)(2,1)S(1)} %get-tuple-element.59), channel_id=1, source_target_pairs={{0,4},{1,5},{2,6},{3,7},{4,8},{5,9},{6,10},{7,11},{8,12},{9,13},{1... | collective-permute-start | bytes 491528 | tf_op jit(solution)/shard_map/ppermute | solution.py:40
  116.4 8.3 %collective-permute-start.18 = (bf16[64,1024]{1,0:T(8,128)(2,1)S(1)}, bf16[64,1024]{1,0:T(8,128)(2,1)S(1)}, u32[]{:S(2)}, u32[]{:S(2)}) collective-permute-start(bf16[64,1024]{1,0:T(8,128)(2,1)S(1)} %shard_map.91.refs_8_.cross_ref), channel_id=1, source_target_pairs={{0,32},{1,33},{2,34},{3,35},{4,36},{5,37},{6,38},{7,39},{8,40},{9,... | collective-permute-start | bytes 393224 | tf_op jit(solution)/shard_map/ppermute | solution.py:40
  116.4 11.2 %collective-permute-start.19 = (bf16[64,1024]{1,0:T(8,128)(2,1)S(1)}, bf16[64,1024]{1,0:T(8,128)(2,1)S(1)}, u32[]{:S(2)}, u32[]{:S(2)}) collective-permute-start(bf16[64,1024]{1,0:T(8,128)(2,1)S(1)} %collective-permute-done.15.refs_9_), channel_id=1, source_target_pairs={{0,32},{1,33},{2,34},{3,35},{4,36},{5,37},{6,38},{7,39},{8,40},{9,... | collective-permute-start | bytes 393224 | tf_op jit(solution)/shard_map/ppermute | solution.py:40
  117.0 10.7 %collective-permute-start.20 = (bf16[64,1024]{1,0:T(8,128)(2,1)S(1)}, bf16[64,1024]{1,0:T(8,128)(2,1)S(1)}, u32[]{:S(2)}, u32[]{:S(2)}) collective-permute-start(bf16[64,1024]{1,0:T(8,128)(2,1)S(1)} %collective-permute-done.16.refs_10_), channel_id=1, source_target_pairs={{0,32},{1,33},{2,34},{3,35},{4,36},{5,37},{6,38},{7,39},{8,40},{9,... | collective-permute-start | bytes 393224 | tf_op jit(solution)/shard_map/ppermute | solution.py:40
  117.1 10.6 %collective-permute-start.21 = (bf16[64,1024]{1,0:T(8,128)(2,1)S(1)}, bf16[64,1024]{1,0:T(8,128)(2,1)S(1)}, u32[]{:S(2)}, u32[]{:S(2)}) collective-permute-start(bf16[64,1024]{1,0:T(8,128)(2,1)S(1)} %collective-permute-done.17.refs_11_), channel_id=1, source_target_pairs={{0,32},{1,33},{2,34},{3,35},{4,36},{5,37},{6,38},{7,39},{8,40},{9,... | collective-permute-start | bytes 393224 | tf_op jit(solution)/shard_map/ppermute | solution.py:40
  124.7 7.0 %collective-permute-start.35 = (f32[128,128]{1,0:T(8,128)S(1)}, f32[128,128]{1,0:T(8,128)S(1)}, u32[]{:S(2)}, u32[]{:S(2)}) collective-permute-start(f32[128,128]{1,0:T(8,128)S(1)} %get-tuple-element.61), channel_id=1, source_target_pairs={{0,224},{1,225},{2,226},{3,227},{4,228},{5,229},{6,230},{7,231},{8... | collective-permute-start | bytes 196616 | tf_op jit(solution)/shard_map/ppermute | solution.py:40
  124.7 7.0 %collective-permute-start.36 = (f32[128,128]{1,0:T(8,128)S(1)}, f32[128,128]{1,0:T(8,128)S(1)}, u32[]{:S(2)}, u32[]{:S(2)}) collective-permute-start(f32[128,128]{1,0:T(8,128)S(1)} %get-tuple-element.62), channel_id=1, source_target_pairs={{0,192},{1,193},{2,194},{3,195},{4,196},{5,197},{6,198},{7,199},{8... | collective-permute-start | bytes 196616 | tf_op jit(solution)/shard_map/ppermute | solution.py:40
  (13 other events, 152.7 us)
